TPU v7x, 32 devices: a whole 2x2x4 slice. The times are simulated.
32 devices in a mesh: groups: 2 (over y), seq: 8 (over z, x), head: 1, sub: 2 (over core).
Axes of the slice: x: 2, y: 2, z: 4, core: 2. Of those that a mesh axis runs over, the one named last changes fastest.
Arguments:
- ssm_input: bfloat16 [2048, 16384], P(('groups', 'seq'), ('head', 'sub')), parts along dimension 0, may hold values from -6 to 6
- gate_input: bfloat16 [2048, 16384], P(('groups', 'seq'), ('head', 'sub')), parts along dimension 0, may hold values from -6 to 6
- step: float32 [2048, 256], P(('groups', 'seq'), ('head', 'sub')), parts along dimension 0, may hold values from 0.5 to 2
- log_decay: float32 [2048, 256], P(('groups', 'seq'), ('head', 'sub')), parts along dimension 0, may hold values from -0.75 to 0
- b_input: bfloat16 [2048, 2048], P(('groups', 'seq'), 'head'), parts along dimension 0, may hold values from -6 to 6
- c_input: bfloat16 [2048, 2048], P(('groups', 'seq'), 'head'), parts along dimension 0, may hold values from -0.01171875 to 0.01171875
- d_skip: float32 [256], P(('head', 'sub')), may hold values from 0.5 to 2
- norm_gain: float32 [16384], P(('head', 'sub')), may hold values from 0.1 to 1.9
- queries: bfloat16 [2048, 8192], P(('groups', 'seq'), ('head', 'sub')), parts along dimension 0, may hold values from -120 to 120
- keys: bfloat16 [2048, 1024], P(('groups', 'seq'), 'head'), parts along dimension 0, may hold values from -5 to 5
- values: bfloat16 [2048, 1024], P(('groups', 'seq'), 'head'), parts along dimension 0, may hold values from -6 to 6
- segment_order: int32 [32], P('groups'), parts along dimension 0, may hold values from 0 to 15, each once
Outputs:
- mixer_out: bfloat16 [2048, 16384], P(('groups', 'seq'), ('head', 'sub')), parts along dimension 0
- attn_out: bfloat16 [2048, 8192], P(('groups', 'seq'), ('head', 'sub')), parts along dimension 0
There are 2 independent parts, one for each index of `groups`. A program takes and returns all parts, laid end to end along the dimension named above; an argument that names none is the same for every part. Nothing has to cross between parts.
Inputs may be any that keep to these rules, and one draw needn't show every extreme that they name: `segment_order`: each number from 0 to 15 appears once.
All inputs are finite; a program needn't handle non-finite values.
Results may differ from a plain program's by a relative error of at most 0.009.
Values may be sent and summed in bfloat16 or wider, within the bound.
No kernel may reach another device: no remote copies, remote signals or barrier semaphores. Data moves between devices by JAX's collectives and lax.ppermute only.
A program may use at most 192 MiB of HBM per device.

v0:
```python
import jax
import jax.numpy as jnp
from jax import lax
from jax.sharding import PartitionSpec as P

SCAN_BLOCK = 128
MIXER_HEADS = 256
STATE = 256
GROUPS_BC = 8
ATT_HEADS = 64
KV_HEADS = 8
ATT_DIM = 128


def entering_2(shard, axis, combine, identity):
    peers, here = (lax.axis_size(axis), lax.axis_index(axis))
    everything = jax.tree.map(
        lambda part, kind: lax.all_gather(part.astype(kind), axis),
        shard,
        (jnp.bfloat16, jnp.bfloat16),
    )
    start = jax.tree.map(
        lambda part, zero: jnp.broadcast_to(jnp.asarray(zero, part.dtype), part.shape),
        shard,
        identity,
    )

    def lap(k, before):
        reached = k < here
        new = combine(
            before, jax.tree.map(lambda part, own: part[k].astype(own.dtype), everything, shard)
        )
        return jax.tree.map(lambda a, b: jnp.where(reached, a, b), new, before)

    return lax.fori_loop(0, peers, lap, start)


def local(
    ssm_input,
    gate_input,
    step,
    log_decay,
    b_input,
    c_input,
    d_skip,
    norm_gain,
    queries,
    keys,
    values,
    segment_order,
):
    row_count = ssm_input.shape[0]
    head_count = step.shape[1]
    head_width = ssm_input.shape[1] // head_count
    group_count = b_input.shape[1] // STATE
    per_group = MIXER_HEADS // GROUPS_BC
    block_count = row_count // SCAN_BLOCK
    highest = lax.Precision.HIGHEST
    sub_index = lax.axis_index("sub")
    head_group = (sub_index * head_count + jnp.arange(head_count, dtype=jnp.int32)) // per_group
    selector = (head_group[:, None] == jnp.arange(group_count, dtype=jnp.int32)[None, :]).astype(
        jnp.float32
    )
    inputs = ssm_input.reshape(block_count, SCAN_BLOCK, head_count, head_width)
    cumulated = jnp.cumsum(log_decay.reshape(block_count, SCAN_BLOCK, head_count), axis=1)
    scaled = (
        inputs.astype(jnp.float32) * step.reshape(block_count, SCAN_BLOCK, head_count)[..., None]
    ).astype(jnp.bfloat16)
    b_blocks = b_input.reshape(block_count, SCAN_BLOCK, group_count, STATE)
    c_blocks = c_input.reshape(block_count, SCAN_BLOCK, group_count, STATE)
    intersections = jnp.einsum(
        "cqgn,ckgn->cgqk", c_blocks, b_blocks, preferred_element_type=jnp.float32
    )
    head_intersections = jnp.einsum("cgqk,hg->cqkh", intersections, selector, precision=highest)
    gaps = cumulated[:, :, None, :] - cumulated[:, None, :, :]
    lower = jnp.tril(jnp.ones((SCAN_BLOCK, SCAN_BLOCK), dtype=bool))
    weights = (jnp.where(lower[None, :, :, None], jnp.exp(gaps), 0.0) * head_intersections).astype(
        jnp.bfloat16
    )
    within = jnp.einsum("cqkh,ckhp->cqhp", weights, scaled, preferred_element_type=jnp.float32)
    ends = cumulated[:, -1, :]
    b_heads = jnp.einsum("cqgn,hg->cqhn", b_blocks.astype(jnp.float32), selector, precision=highest)
    weighted_b = (jnp.exp(ends[:, None, :] - cumulated)[..., None] * b_heads).astype(jnp.bfloat16)
    contributions = jnp.einsum(
        "ckhn,ckhp->chnp", weighted_b, scaled, preferred_element_type=jnp.float32
    )
    factors = jnp.exp(ends)
    running = jnp.zeros(contributions.shape[1:], jnp.float32)
    local_states = [running]
    running = factors[0][:, None, None] * running + contributions[0]
    through = jnp.exp(jnp.sum(ends, axis=0))
    before = jnp.exp(jnp.cumsum(ends, axis=0) - ends)

    def combine(earlier, later):
        return (earlier[0] * later[0], later[0][:, None, None] * earlier[1] + later[1])

    identity = (jnp.ones_like(through), jnp.zeros_like(running))
    arriving = entering_2((through, running), "seq", combine, identity)[1]
    entering = jnp.stack(local_states) + before[:, :, None, None] * arriving[None]
    c_heads = jnp.einsum(
        "cqgn,hg->cqhn", c_blocks.astype(jnp.float32), selector, precision=highest
    ).astype(jnp.bfloat16)
    carried = jnp.einsum(
        "cqhn,chnp->cqhp",
        c_heads,
        entering.astype(jnp.bfloat16),
        preferred_element_type=jnp.float32,
    )
    carried = carried * jnp.exp(cumulated)[..., None]
    mixed = within + carried + d_skip[None, None, :, None] * inputs.astype(jnp.float32)
    gates = gate_input.reshape(block_count, SCAN_BLOCK, head_count, head_width).astype(jnp.float32)
    gated = mixed * jax.nn.silu(gates)
    mean_square = jnp.sum(gated * gated, axis=3) / head_width
    normed = (
        gated
        * lax.rsqrt(mean_square + 1e-05)[..., None]
        * norm_gain.reshape(head_count, head_width)
    )
    mixer_out = normed.astype(jnp.bfloat16).reshape(row_count, head_count * head_width)
    query_count = queries.shape[1] // ATT_DIM
    kv_count = keys.shape[1] // ATT_DIM
    ratio = ATT_HEADS // KV_HEADS
    used_heads = max(1, query_count // ratio)
    per_used = query_count // used_heads
    first_head = sub_index * query_count // ratio
    query_heads = queries.reshape(row_count, used_heads, per_used, ATT_DIM)
    seg_len = row_count // 2
    own_rows = lax.axis_index("seq") * row_count + jnp.arange(row_count, dtype=jnp.int32)
    query_pos = segment_order[own_rows // seg_len] * seg_len + own_rows % seg_len
    scale = ATT_DIM ** (-0.5)
    key_rows = lax.all_gather(keys, "seq", axis=0, tiled=True)
    value_rows = lax.all_gather(values, "seq", axis=0, tiled=True)
    piece_len = key_rows.shape[0]
    key_index = jnp.arange(piece_len, dtype=jnp.int32)
    key_pos = segment_order[key_index // seg_len] * seg_len + key_index % seg_len
    key_piece = lax.dynamic_slice_in_dim(
        key_rows.reshape(piece_len, kv_count, ATT_DIM), first_head, used_heads, 1
    )
    value_piece = lax.dynamic_slice_in_dim(
        value_rows.reshape(piece_len, kv_count, ATT_DIM), first_head, used_heads, 1
    )
    peak = jnp.full((row_count, used_heads, per_used), -1e30, jnp.float32)
    scores = (
        jnp.einsum("tgrd,sgd->tgrs", query_heads, key_piece, preferred_element_type=jnp.float32)
        * scale
    )
    visible = key_pos[None, :] <= query_pos[:, None]
    scores = jnp.where(visible[:, None, None, :], scores, -jnp.inf)
    new_peak = jnp.maximum(peak, jnp.max(scores, axis=-1))
    expos = jnp.exp(scores - new_peak[..., None])
    new_totals = jnp.sum(expos, axis=-1)
    update = jnp.einsum(
        "tgrs,sgd->tgrd",
        expos.astype(jnp.bfloat16),
        value_piece,
        preferred_element_type=jnp.float32,
    )
    attn_out = (
        (update / new_totals[..., None])
        .astype(jnp.bfloat16)
        .reshape(row_count, query_count * ATT_DIM)
    )
    return (mixer_out, attn_out)


def solution(mesh):
    placed = (
        P(("groups", "seq"), ("head", "sub")),
        P(("groups", "seq"), ("head", "sub")),
        P(("groups", "seq"), ("head", "sub")),
        P(("groups", "seq"), ("head", "sub")),
        P(("groups", "seq"), "head"),
        P(("groups", "seq"), "head"),
        P(("head", "sub")),
        P(("head", "sub")),
        P(("groups", "seq"), ("head", "sub")),
        P(("groups", "seq"), "head"),
        P(("groups", "seq"), "head"),
        P("groups"),
    )
    return jax.shard_map(
        local,
        mesh=mesh,
        in_specs=placed,
        out_specs=(P(("groups", "seq"), ("head", "sub")), P(("groups", "seq"), ("head", "sub"))),
        check_vma=False,
    )
```

profile of v0, /device:TPU:18, one launch (start us, length us, event | category | flops | bytes accessed | tf_op | source)
XLA Modules:
  0.0 996.5 jit_solution(4848412685608290985)
XLA Ops:
  20.2 11.7 %add_convert_fusion = bf16[128,256,64]{1,2,0:T(8,128)(2,1)} fusion(f32[128]{0:T(128)S(1)} %get-tuple-element.149, bf16[128,128,256]{2,1,0:T(8,128)(2,1)S(1)} %fusion.13, f32[128,128,64]{0,2,1:T(8,128)S(1)} %bitcast.208, f32[128,128]{0,1:T(8,128)S(1)} %copy.48), kind=kOutput, calls=%fused_computation.17 | convolution fusion | flops 543162368 | bytes 16843264 | tf_op jit(solution)/shard_map/ckhn,ckhp->chnp/dot_general | solution.py:84
  32.2 14.8 %all-gather = bf16[8,1,128]{2,1,0:T(2,128)(2,1)S(1)} all-gather(bf16[1,1,128]{2,1,0:T(2,128)(2,1)S(1)} %get-tuple-element.151), channel_id=2, replica_groups=mesh['groups'=2,'seq'=8,'head'=1,'sub'=2] {'seq'}, dimensions={0}, use_global_device_ids=true | all-gather | bytes 2304 | tf_op jit(solution)/shard_map/all_gather | solution.py:18
  47.4 10.4 %multiply_convert_fusion.2 = bf16[128,128,128]{2,1,0:T(8,128)(2,1)} fusion(f32[128,128]{1,0:T(8,128)S(1)} %bitcast.224, pred[128,128]{1,0:T(8,128)(4,1)S(1)} %iota_compare_fusion, f32[8,128,128]{2,1,0:T(8,128)S(1)} %fusion.31, s32[128]{0:T(128)S(1)} %and_select_fusion.3), kind=kOutput, calls=%fused_computation.19 | convolution fusion | flops 209716224 | bytes 4801024 | tf_op jit(solution)/shard_map/cgqk,hg->cqkh/dot_general | solution.py:74
  70.7 10.8 %fusion.48 = s32[128]{0:T(128)S(1)} fusion(s32[]{:T(128)} %bitcast.31, s32[]{:T(128)} %bitcast.32, s32[]{:T(128)} %bitcast.33, s32[]{:T(128)} %bitcast.34, s32[]{:T(128)} %bitcast.35, s32[]{:T(128)} %bitcast.37, s32[]{:T(128)} %bitcast.36, s32[]{:T(128)} %bitcast.22, s32[]{:T(128)} %bitcast.23, s32[]{:T(128)} %bitcast.24, s32[]{:T(128)} %bitcast.25, ...), kind=kLoop, calls=%fused_computation.110 | loop fusion | flops 8064 | bytes 580 | tf_op jit(solution)/shard_map/add | solution.py:129
  110.0 8.8 fusion.4
  118.9 10.2 %fusion.2 = f32[128,4,8]{0,2,1:T(8,128)S(1)} fusion(f32[4,1024,128,8]{2,1,3,0:T(8,128)} %get-tuple-element.171, f32[128,4,8]{0,2,1:T(8,128)S(1)} %broadcast_maximum_fusion, pred[128,1024]{0,1:T(8,128)(4,1)S(1)} %broadcast_compare_fusion), kind=kLoop, calls=%fused_computation.9 | loop fusion | flops 16773120 | bytes 16941056 | tf_op jit(solution)/shard_map/reduce_sum | solution.py:151
  129.0 9.7 fusion.21
  140.1 608.3 %all-gather.10.cloned.1.call-done = bf16[1024,256,64]{1,2,0:T(8,128)(2,1)} async-done(((bf16[128,256,64]{1,2,0:T(8,128)(2,1)}), bf16[1024,256,64]{1,2,0:T(8,128)(2,1)}) %all-gather.10.cloned.1.call-update) | async-done | bytes 33554448 | tf_op jit(solution)/shard_map/all_gather | solution.py:18
  748.4 215.1 %while.14 = (s32[]{:T(128)}, f32[128,256,64]{2,1,0:T(8,128)}, s32[]{:T(128)}, bf16[8,128]{1,0:T(8,128)(2,1)S(1)}, bf16[8,128,256,64]{2,3,1,0:T(8,128)(2,1)}, /*index=5*/s32[]{:T(128)}, s32[]{:T(128)}) while((s32[]{:T(128)}, f32[128,256,64]{2,1,0:T(8,128)}, s32[]{:T(128)}, bf16[8,128]{1,0:T(8,128)(2,1)S(1)}, ...), condition=%wide.region_2.3_spmd.clone, body=%wide.region_1.2_spmd.clone.sunk | while | flops 10485892 | bytes 37750120 | solution.py:35
  753.2 8.4 copy.105
  761.5 10.8 %fusion.61 = f32[128,256,64]{2,1,0:T(8,128)} fusion(f32[128,256,64]{2,1,0:T(8,128)} %get-tuple-element.211, bf16[1,128,256,64]{3,2,1,0:T(8,128)(2,1)} %copy.105, f32[128]{0:T(128)S(1)} %bitcast_convert_fusion.2, pred[]{:T(512)S(6)} %compare.285, pred[]{:T(512)S(6)} %lt.97), kind=kLoop, calls=%fused_computation.1.clone.1 | loop fusion | flops 10485760 | bytes 20972034 | tf_op jit(solution)/shard_map/while/body/eval_jaxpr/jit(_where)/select_n | solution.py:33
  777.1 8.4 copy.105
  785.5 14.2 %fusion.61 = f32[128,256,64]{2,1,0:T(8,128)} fusion(f32[128,256,64]{2,1,0:T(8,128)} %get-tuple-element.211, bf16[1,128,256,64]{3,2,1,0:T(8,128)(2,1)} %copy.105, f32[128]{0:T(128)S(1)} %bitcast_convert_fusion.2, pred[]{:T(512)S(6)} %compare.285, pred[]{:T(512)S(6)} %lt.97), kind=kLoop, calls=%fused_computation.1.clone.1 | loop fusion | flops 10485760 | bytes 20972034 | tf_op jit(solution)/shard_map/while/body/eval_jaxpr/jit(_where)/select_n | solution.py:33
  804.4 8.4 copy.105
  812.8 14.2 %fusion.61 = f32[128,256,64]{2,1,0:T(8,128)} fusion(f32[128,256,64]{2,1,0:T(8,128)} %get-tuple-element.211, bf16[1,128,256,64]{3,2,1,0:T(8,128)(2,1)} %copy.105, f32[128]{0:T(128)S(1)} %bitcast_convert_fusion.2, pred[]{:T(512)S(6)} %compare.285, pred[]{:T(512)S(6)} %lt.97), kind=kLoop, calls=%fused_computation.1.clone.1 | loop fusion | flops 10485760 | bytes 20972034 | tf_op jit(solution)/shard_map/while/body/eval_jaxpr/jit(_where)/select_n | solution.py:33
  831.7 8.4 copy.105
  840.1 14.2 %fusion.61 = f32[128,256,64]{2,1,0:T(8,128)} fusion(f32[128,256,64]{2,1,0:T(8,128)} %get-tuple-element.211, bf16[1,128,256,64]{3,2,1,0:T(8,128)(2,1)} %copy.105, f32[128]{0:T(128)S(1)} %bitcast_convert_fusion.2, pred[]{:T(512)S(6)} %compare.285, pred[]{:T(512)S(6)} %lt.97), kind=kLoop, calls=%fused_computation.1.clone.1 | loop fusion | flops 10485760 | bytes 20972034 | tf_op jit(solution)/shard_map/while/body/eval_jaxpr/jit(_where)/select_n | solution.py:33
  859.0 8.4 copy.105
  867.4 14.2 %fusion.61 = f32[128,256,64]{2,1,0:T(8,128)} fusion(f32[128,256,64]{2,1,0:T(8,128)} %get-tuple-element.211, bf16[1,128,256,64]{3,2,1,0:T(8,128)(2,1)} %copy.105, f32[128]{0:T(128)S(1)} %bitcast_convert_fusion.2, pred[]{:T(512)S(6)} %compare.285, pred[]{:T(512)S(6)} %lt.97), kind=kLoop, calls=%fused_computation.1.clone.1 | loop fusion | flops 10485760 | bytes 20972034 | tf_op jit(solution)/shard_map/while/body/eval_jaxpr/jit(_where)/select_n | solution.py:33
  894.7 14.2 %fusion.61 = f32[128,256,64]{2,1,0:T(8,128)} fusion(f32[128,256,64]{2,1,0:T(8,128)} %get-tuple-element.211, bf16[1,128,256,64]{3,2,1,0:T(8,128)(2,1)} %copy.105, f32[128]{0:T(128)S(1)} %bitcast_convert_fusion.2, pred[]{:T(512)S(6)} %compare.285, pred[]{:T(512)S(6)} %lt.97), kind=kLoop, calls=%fused_computation.1.clone.1 | loop fusion | flops 10485760 | bytes 20972034 | tf_op jit(solution)/shard_map/while/body/eval_jaxpr/jit(_where)/select_n | solution.py:33
  922.0 14.2 %fusion.61 = f32[128,256,64]{2,1,0:T(8,128)} fusion(f32[128,256,64]{2,1,0:T(8,128)} %get-tuple-element.211, bf16[1,128,256,64]{3,2,1,0:T(8,128)(2,1)} %copy.105, f32[128]{0:T(128)S(1)} %bitcast_convert_fusion.2, pred[]{:T(512)S(6)} %compare.285, pred[]{:T(512)S(6)} %lt.97), kind=kLoop, calls=%fused_computation.1.clone.1 | loop fusion | flops 10485760 | bytes 20972034 | tf_op jit(solution)/shard_map/while/body/eval_jaxpr/jit(_where)/select_n | solution.py:33
  940.9 8.4 copy.105
  949.3 14.2 %fusion.61 = f32[128,256,64]{2,1,0:T(8,128)} fusion(f32[128,256,64]{2,1,0:T(8,128)} %get-tuple-element.211, bf16[1,128,256,64]{3,2,1,0:T(8,128)(2,1)} %copy.105, f32[128]{0:T(128)S(1)} %bitcast_convert_fusion.2, pred[]{:T(512)S(6)} %compare.285, pred[]{:T(512)S(6)} %lt.97), kind=kLoop, calls=%fused_computation.1.clone.1 | loop fusion | flops 10485760 | bytes 20972034 | tf_op jit(solution)/shard_map/while/body/eval_jaxpr/jit(_where)/select_n | solution.py:33
  963.5 20.7 %multiply_reduce_fusion = (f32[128,128]{0,1:T(8,128)S(1)}, f32[1,128,128,64]{1,3,2,0:T(8,128)}) fusion(f32[1,128,128,64]{1,3,2,0:T(8,128)} %bitcast.210, f32[1,128,128,64]{1,3,2,0:T(8,128)} %bitcast.207, f32[128]{0:T(128)S(1)} %copy-done.11, f32[128,128]{0,1:T(8,128)S(1)} %copy.57, bf16[128,128,256]{2,1,0:T(8,128)(2,1)} %convert_bitcast_fusion, ...), kind=kOutput, calls=%fused_computation.28 | convolution fusion | flops 552583168 | bytes 33686528 | tf_op jit(solution)/shard_map/cqhn,chnp->cqhp/dot_general | solution.py:103
  (92 shorter events, 116.7 us)
Async XLA Ops:
  7.2 9.3 copy-start.8
  7.2 9.4 copy-start.9
  7.2 96.0 %all-gather.6.cloned.1.call-start = ((), (), s32[]{:S(2)}) async-start(), calls=%async_computation | async-start | bytes 2359296 | tf_op jit(solution)/shard_map/all_gather | solution.py:132
  7.9 102.1 %all-gather.8.cloned.1.call-start = ((), (), s32[]{:S(2)}) async-start(), calls=%async_computation.1 | async-start | bytes 2359296 | tf_op jit(solution)/shard_map/all_gather | solution.py:131
  9.8 738.6 %all-gather.10.cloned.1.call-start = ((), (), s32[]{:S(2)}) async-start(), calls=%async_computation.2 | async-start | bytes 37748736 | tf_op jit(solution)/shard_map/all_gather | solution.py:18
  16.7 3.4 copy-start
  20.2 11.8 %copy-start.6 = (bf16[128,4096]{1,0:T(8,128)(2,1)S(1)}, bf16[128,4096]{1,0:T(8,128)(2,1)}, u32[]{:S(2)}) copy-start(bf16[128,4096]{1,0:T(8,128)(2,1)} %param.22) | copy-start | bytes 3145732
  20.2 26.9 %copy-start.4 = (bf16[128,2048]{1,0:T(8,128)(2,1)S(1)}, bf16[128,2048]{1,0:T(8,128)(2,1)}, u32[]{:S(2)}) copy-start(bf16[128,2048]{1,0:T(8,128)(2,1)} %param.18) | copy-start | bytes 1572868
  20.2 26.9 %copy-start.5 = (bf16[128,2048]{1,0:T(8,128)(2,1)S(1)}, bf16[128,2048]{1,0:T(8,128)(2,1)}, u32[]{:S(2)}) copy-start(bf16[128,2048]{1,0:T(8,128)(2,1)} %param.19) | copy-start | bytes 1572868
  47.4 19.2 %copy-start.3 = (bf16[128,8192]{1,0:T(8,128)(2,1)S(1)}, bf16[128,8192]{1,0:T(8,128)(2,1)}, u32[]{:S(2)}) copy-start(bf16[128,8192]{1,0:T(8,128)(2,1)} %param.15) | copy-start | bytes 6291460
  57.8 11.8 %copy-start.10 = (f32[8192]{0:T(1024)S(1)}, f32[8192]{0:T(1024)}, u32[]{:S(2)}) copy-start(f32[8192]{0:T(1024)} %param.21) | copy-start | bytes 98308
  57.8 12.2 %copy-start.7 = (s32[16]{0:T(128)S(1)}, s32[16]{0:T(128)}, u32[]{:S(2)}) copy-start(s32[16]{0:T(128)} %param.25) | copy-start | bytes 196
  69.6 28.6 %copy-start.1 = (f32[128,8192]{0,1:T(8,128)S(1)}, f32[128,8192]{0,1:T(8,128)}, u32[]{:S(2)}) copy-start(f32[128,8192]{0,1:T(8,128)} %convert_element_type.142) | copy-start | bytes 12582916
  69.6 28.6 %copy-start.2 = (bf16[128,128,128]{1,0,2:T(8,128)(2,1)S(1)}, bf16[128,128,128]{1,0,2:T(8,128)(2,1)}, u32[]{:S(2)}) copy-start(bf16[128,128,128]{1,0,2:T(8,128)(2,1)} %copy.52) | copy-start | bytes 12582916
  748.4 215.1 %copy-start.11 = (f32[128]{0:T(128)S(1)}, f32[128]{0:T(128)}, u32[]{:S(2)}) copy-start(f32[128]{0:T(128)} %param.20) | copy-start | bytes 1540
Sparse Core Ops, SparseCore 0:
  10.1 48.7 all-gather.5
  61.5 48.4 all-gather.7
  111.6 636.7 all-gather.9
where the time goes:
time: 1000 us; the launch traced here: 997 us
  waiting for transfers between devices  613 us (61%)
  other arithmetic  147 us (15%)
  local copies, waits for them, and re-layouts  131 us (13%)
  matrix products  76.5 us (8%)
  blocking collectives  14.8 us (1%)
  between operations  14 us (1%)
    all_gather x1, waiting for transfers between devices, entering_2(): lax.all_gather(part.astype(kind), axis)  608 us
    select_n x8, other arithmetic, lap(): return jax.tree.map(lambda a, b: jnp.where(reached, a, b), new, before)  110 us
    dynamic_slice x16, local copies, waits for them, and re-layouts, lap(): part[k].astype(own.dtype)  105 us
    dot_general x1, matrix products, local(): jnp.einsum('cqhn,chnp->cqhp', c_heads, entering.astype(jnp.bfloat16), pre...  20.7 us
  transfers between devices with their start and end apart: 3, of which 2 were waited for; matrix products, arithmetic and copies ran while one was open for 11% of the time, Pallas kernels for 0%

commit v1 on v0

v1 whole, which is shorter than its diff:
```python
import functools
import math
import jax
import jax.numpy as jnp
from jax import lax
from jax.experimental import pallas as pl
from jax.experimental.pallas import tpu as pltpu
from jax.sharding import PartitionSpec as P

SCAN_BLOCK = 128
MIXER_HEADS = 256
STATE = 256
GROUPS_BC = 8
ATT_HEADS = 64
KV_HEADS = 8
ATT_DIM = 128
WIDTH = 64
PER_GROUP = MIXER_HEADS // GROUPS_BC
CHUNKS = 4
F32 = jnp.float32
BF16 = jnp.bfloat16


def dot(a, b, dims=((1,), (0,))):
    return lax.dot_general(a, b, (dims, ((), ())), preferred_element_type=F32)


def pair_columns(cols, j):
    lane = lax.broadcasted_iota(jnp.int32, (cols.shape[0], 2 * WIDTH), 1)
    return jnp.where(lane < WIDTH, cols[:, 2 * j : 2 * j + 1], cols[:, 2 * j + 1 : 2 * j + 2])


def expand(cols):
    return jnp.concatenate([pair_columns(cols, j) for j in range(cols.shape[1] // 2)], axis=1)


def call(body, grid, in_specs, out_specs, out_shape, scratch=(), aliases={}):
    return pl.pallas_call(
        body,
        out_shape=out_shape,
        grid_spec=pltpu.PrefetchScalarGridSpec(
            num_scalar_prefetch=1,
            grid=grid,
            in_specs=in_specs,
            out_specs=out_specs,
            scratch_shapes=list(scratch),
        ),
        input_output_aliases=aliases,
    )


def shaped(shape, dtype):
    return jax.ShapeDtypeStruct(shape, dtype)


def whole(shape):
    zeros = (0,) * len(shape)
    return pl.BlockSpec(shape, lambda *_: zeros)


def scalars_body(_, step_ref, decay_ref, stepb, cumb, wb, endb, cumt):
    rows, heads = step_ref.shape
    chunks, width = stepb.shape[0], stepb.shape[2]
    decay = decay_ref[...]
    lower = (
        lax.broadcasted_iota(jnp.int32, (rows, rows), 0)
        >= lax.broadcasted_iota(jnp.int32, (rows, rows), 1)
    ).astype(F32)
    cum = lax.dot_general(
        lower, decay, (((1,), (0,)), ((), ())), precision=lax.Precision.HIGHEST,
        preferred_element_type=F32,
    )
    end = cum[rows - 1 : rows, :]
    w = jnp.exp(end - cum)
    factor = jnp.exp(end)
    cumt[...] = cum.T
    for j in range(chunks):
        cut = slice(j * width, (j + 1) * width)
        stepb[j] = step_ref[:, cut]
        cumb[j] = cum[:, cut]
        wb[j] = w[:, cut]
        endb[j] = factor[:, cut]


def weighted_inputs(x, step, w):
    parts = []
    for j in range(step.shape[1] // 2):
        cut = slice(j * 2 * WIDTH, (j + 1) * 2 * WIDTH)
        scaled = (x[:, cut].astype(F32) * pair_columns(step, j)).astype(BF16)
        parts.append((scaled.astype(F32) * pair_columns(w, j)).astype(BF16))
    return jnp.concatenate(parts, axis=1)


def send_body(_, x_ref, step_ref, w_ref, out_ref):
    out_ref[...] = weighted_inputs(x_ref[...], step_ref[0], w_ref[0])


def plane_body(
    meta, x_ref, step_ref, w_ref, end_ref, b_own, c_own, sd_oth, b_oth, c_oth, end_oth,
    total_ref, send_ref, inner_ref,
):
    first = meta[0] == 0
    own = dot(b_own[...], weighted_inputs(x_ref[...], step_ref[0], w_ref[0]), ((0,), (0,)))
    oth = dot(b_oth[...], sd_oth[...], ((0,), (0,)))
    d_own, d_oth = expand(end_ref[0]), expand(end_oth[0])
    one = jnp.ones_like(d_own)
    total = own * jnp.where(first, d_oth, one) + oth * jnp.where(first, one, d_own)
    total_ref[...] = total
    send_ref[...] = total.astype(BF16)
    earlier = jnp.where(first, own, oth).astype(BF16)
    c_later = jnp.where(first, c_oth[...].astype(F32), c_own[...].astype(F32)).astype(BF16)
    inner_ref[...] = dot(c_later, earlier)


def hop_body(_, recv_ref, total_ref, end_ref, end_oth, out_ref):
    d = expand(end_ref[0] * end_oth[0])
    out_ref[...] = (d * recv_ref[...].astype(F32) + total_ref[...]).astype(BF16)


def carried_body(hops, meta, *refs):
    recvs = refs[:hops]
    c_own, c_oth, inner_ref, end_ref, end_oth, own_ref, oth_ref = refs[hops:]
    first = meta[0] == 0
    state = recvs[0][...].astype(F32)
    for r in recvs[1:]:
        state = state + r[...].astype(F32)
    state = state.astype(BF16)
    d_own, d_oth = expand(end_ref[0]), expand(end_oth[0])
    one = jnp.ones_like(d_own)
    inner = inner_ref[...]
    zero = jnp.zeros_like(inner)
    own = dot(c_own[...], state) * jnp.where(first, one, d_oth) + jnp.where(first, zero, inner)
    oth = dot(c_oth[...], state) * jnp.where(first, d_own, one) + jnp.where(first, inner, zero)
    own_ref[...] = own.astype(BF16)
    oth_ref[...] = oth.astype(BF16)


def within_body(_, x_ref, step_ref, cum_ref, cumt_ref, skip_ref, b_ref, c_ref, out_ref):
    rows = x_ref.shape[0]
    above = lax.broadcasted_iota(jnp.int32, (rows, rows), 0) < lax.broadcasted_iota(
        jnp.int32, (rows, rows), 1
    )
    inter = jnp.where(above, 0.0, dot(c_ref[...], b_ref[...], ((1,), (1,))))
    lane = lax.broadcasted_iota(jnp.int32, (rows, 2 * WIDTH), 1)
    step, cum, skip = step_ref[0], cum_ref[0], skip_ref[0]
    for j in range(step.shape[1] // 2):
        cut = slice(j * 2 * WIDTH, (j + 1) * 2 * WIDTH)
        x = x_ref[:, cut].astype(F32)
        scaled = x * pair_columns(step, j)
        weights = []
        for h in (2 * j, 2 * j + 1):
            gap = jnp.minimum(cum[:, h : h + 1] - cumt_ref[0, h : h + 1, :], 0.0)
            weights.append((jnp.exp(gap) * inter).astype(BF16))
        stacked = jnp.concatenate(
            [
                jnp.where(lane < WIDTH, scaled, 0.0).astype(BF16),
                jnp.where(lane < WIDTH, 0.0, scaled).astype(BF16),
            ],
            axis=0,
        )
        out_ref[:, cut] = dot(jnp.concatenate(weights, axis=1), stacked) + x * pair_columns(skip, j)


def gate_body(meta, mixed_ref, carried_ref, gate_ref, cum_ref, gain_ref, *rest):
    out_ref = rest[-1]
    cum = jnp.exp(cum_ref[0])
    size = 2 * WIDTH
    same = (
        lax.broadcasted_iota(jnp.int32, (size, size), 0) // WIDTH
        == lax.broadcasted_iota(jnp.int32, (size, size), 1) // WIDTH
    )
    mean = jnp.where(same, 1.0 / WIDTH, 0.0).astype(BF16)
    for j in range(cum.shape[1] // 2):
        cut = slice(j * size, (j + 1) * size)
        mixed = mixed_ref[:, cut] + carried_ref[:, cut].astype(F32) * pair_columns(cum, j)
        gate = gate_ref[:, cut].astype(F32)
        gated = mixed * (gate / (1.0 + jnp.exp(-gate)))
        square = gated * gated
        high = square.astype(BF16)
        low = (square - high.astype(F32)).astype(BF16)
        mean_square = dot(high, mean) + dot(low, mean)
        out_ref[:, cut] = (gated * lax.rsqrt(mean_square + 1e-05) * gain_ref[:, cut]).astype(BF16)


def attend_body(per_used, _, q_ref, *refs):
    keys, values = refs[0:2], refs[2:4]
    qpos_ref, kpos_ref, out_ref, bias = refs[4:]

    @pl.when(pl.program_id(0) == 0)
    def _():
        bias[...] = jnp.where(kpos_ref[...] <= qpos_ref[...], 0.0, -jnp.inf)

    shape = (-1, ATT_DIM)
    key = jnp.concatenate([k[...].reshape(shape) for k in keys], axis=0)
    value = jnp.concatenate([v[...].reshape(shape) for v in values], axis=0)
    factor = ATT_DIM ** (-0.5) * math.log2(math.e)
    for r in range(per_used):
        cut = slice(r * ATT_DIM, (r + 1) * ATT_DIM)
        scores = dot(q_ref[:, cut], key, ((1,), (1,))) + bias[...]
        peak = jnp.max(scores, axis=1, keepdims=True)
        expos = jnp.exp2((scores - peak) * factor)
        total = jnp.sum(expos, axis=1, keepdims=True)
        out_ref[:, cut] = (dot(expos.astype(BF16), value) / total).astype(BF16)


def local(
    ssm_input, gate_input, step, log_decay, b_input, c_input, d_skip, norm_gain,
    queries, keys, values, segment_order,
):
    rows, heads = step.shape
    peers, here = lax.axis_size("seq"), lax.axis_index("seq")
    sub_index = lax.axis_index("sub")
    planes = peers // 2
    side, plane = here % 2, here // 2
    half = heads // 2
    count = CHUNKS
    per_chunk = half // count
    wide = per_chunk * WIDTH
    chunks = 2 * count
    swap = [(i, i ^ 1) for i in range(peers)]
    up = [(i, i + 2) for i in range(peers - 2)]
    down = [(i + 2, i) for i in range(peers - 2)]

    query_count = queries.shape[1] // ATT_DIM
    ratio = ATT_HEADS // KV_HEADS
    used_heads = max(1, query_count // ratio)
    per_used = query_count // used_heads
    first_head = sub_index * query_count // ratio
    kv_wide = used_heads * ATT_DIM
    start = first_head * ATT_DIM
    pack = jnp.concatenate(
        [
            lax.dynamic_slice_in_dim(keys, start, kv_wide, 1),
            lax.dynamic_slice_in_dim(values, start, kv_wide, 1),
        ],
        axis=1,
    )
    gathered = jnp.zeros((planes + 1,) + pack.shape, BF16)
    gathered = lax.dynamic_update_slice_in_dim(gathered, pack[None], plane, 0)
    rising = falling = pack
    for i in range(1, planes):
        rising = lax.ppermute(rising, "seq", up)
        falling = lax.ppermute(falling, "seq", down)
        gathered = lax.dynamic_update_slice_in_dim(
            gathered, rising[None], jnp.where(plane >= i, plane - i, planes), 0
        )
        gathered = lax.dynamic_update_slice_in_dim(
            gathered, falling[None], jnp.where(plane + i < planes, plane + i, planes), 0
        )
    other_side = lax.ppermute(gathered[:planes], "seq", swap)

    stepb, cumb, wb, endb, cumt = call(
        scalars_body,
        (1,),
        [whole((rows, heads))] * 2,
        [whole((chunks, rows, per_chunk))] * 3 + [whole((chunks, 1, per_chunk)), whole((heads, rows))],
        [shaped((chunks, rows, per_chunk), F32)] * 3
        + [shaped((chunks, 1, per_chunk), F32), shaped((heads, rows), F32)],
    )(jnp.zeros((1,), jnp.int32), step, log_decay)

    base = sub_index * heads
    group_of = lambda chunk: (base + chunk * per_chunk) // PER_GROUP
    groups_half = max(1, half // PER_GROUP)
    given = (1 - side) * half
    bc_start = ((base + given) // PER_GROUP) * STATE
    bc_oth = lax.ppermute(
        jnp.concatenate(
            [
                lax.dynamic_slice_in_dim(b_input, bc_start, groups_half * STATE, 1),
                lax.dynamic_slice_in_dim(c_input, bc_start, groups_half * STATE, 1),
            ],
            axis=1,
        ),
        "seq",
        swap,
    )
    end_oth = lax.ppermute(
        lax.dynamic_slice_in_dim(endb, (1 - side) * count, count, 0), "seq", swap
    )

    narrow = lambda size=rows: pl.BlockSpec((1, size, per_chunk), lambda i, m: (m[1], 0, 0))
    columns = pl.BlockSpec((rows, wide), lambda i, m: (0, m[1]))
    sd_oth = []
    for c in range(count):
        meta = jnp.stack([side, (1 - side) * count + c])
        sd = call(
            send_body, (1,), [columns, narrow(), narrow()], whole((rows, wide)),
            shaped((rows, wide), BF16),
        )(meta, ssm_input, stepb, wb)
        sd_oth.append(lax.ppermute(sd, "seq", swap))

    group_block = pl.BlockSpec((rows, STATE), lambda i, m: (0, m[2]))
    metas, totals, sends, inners = [], [], [], []
    for c in range(count):
        mine = side * count + c
        meta = jnp.stack([side, mine, group_of(mine)])
        in_half = c * per_chunk // PER_GROUP
        oth_block = lambda at: pl.BlockSpec((rows, STATE), lambda i, m, at=at: (0, at))
        oth_end = pl.BlockSpec((1, 1, per_chunk), lambda i, m, c=c: (c, 0, 0))
        total, send, inner = call(
            plane_body,
            (1,),
            [
                columns, narrow(), narrow(), narrow(1), group_block, group_block,
                whole((rows, wide)), oth_block(in_half), oth_block(groups_half + in_half), oth_end,
            ],
            [whole((STATE, wide)), whole((STATE, wide)), whole((rows, wide))],
            [shaped((STATE, wide), F32), shaped((STATE, wide), BF16), shaped((rows, wide), F32)],
        )(meta, ssm_input, stepb, wb, endb, b_input, c_input, sd_oth[c], bc_oth, bc_oth, end_oth)
        metas.append((meta, in_half, oth_block, oth_end))
        totals.append(total)
        sends.append(send)
        inners.append(inner)

    received = [[] for _ in range(count)]
    for wave in range(count + planes - 2):
        for h in range(planes - 1):
            c = wave - h
            if not 0 <= c < count:
                continue
            meta, _, _, oth_end = metas[c]
            got = lax.ppermute(sends[c], "seq", [(2 * h + x, 2 * h + 2 + x) for x in range(2)])
            received[c].append(got)
            if h < planes - 2:
                sends[c] = call(
                    hop_body,
                    (1,),
                    [whole((STATE, wide)), whole((STATE, wide)), narrow(1), oth_end],
                    whole((STATE, wide)),
                    shaped((STATE, wide), BF16),
                )(meta, got, totals[c], endb, end_oth)

    skips = d_skip.reshape(chunks, 1, per_chunk)
    mixed = call(
        within_body,
        (chunks,),
        [
            pl.BlockSpec((rows, wide), lambda i, m: (0, i)),
            pl.BlockSpec((1, rows, per_chunk), lambda i, m: (i, 0, 0)),
            pl.BlockSpec((1, rows, per_chunk), lambda i, m: (i, 0, 0)),
            pl.BlockSpec((1, per_chunk, rows), lambda i, m: (i, 0, 0)),
            pl.BlockSpec((1, 1, per_chunk), lambda i, m: (i, 0, 0)),
            pl.BlockSpec((rows, STATE), lambda i, m: (0, m[i])),
            pl.BlockSpec((rows, STATE), lambda i, m: (0, m[i])),
        ],
        pl.BlockSpec((rows, wide), lambda i, m: (0, i)),
        shaped((rows, heads * WIDTH), F32),
    )(
        group_of(jnp.arange(chunks, dtype=jnp.int32)), ssm_input, stepb, cumb,
        cumt.reshape(chunks, per_chunk, rows), skips, b_input, c_input,
    )

    gains = norm_gain.reshape(1, heads * WIDTH)
    mixer_out = None

    def finish(mixer_out, chunk, carried):
        specs = [
            columns, whole((rows, wide)), columns, narrow(),
            pl.BlockSpec((1, wide), lambda i, m: (0, m[1])),
        ]
        args = [mixed, carried, gate_input, cumb, gains]
        aliases = {}
        if mixer_out is not None:
            specs.append(pl.BlockSpec(memory_space=pl.ANY))
            args.append(mixer_out)
            aliases = {len(args): 0}
        return call(
            gate_body, (1,), specs, columns, shaped((rows, heads * WIDTH), BF16), aliases=aliases
        )(jnp.stack([side, chunk]), *args)

    back = []
    for c in range(count):
        meta, in_half, oth_block, oth_end = metas[c]
        own, oth = call(
            functools.partial(carried_body, planes - 1),
            (1,),
            [whole((STATE, wide))] * (planes - 1)
            + [group_block, oth_block(groups_half + in_half), whole((rows, wide)), narrow(1), oth_end],
            [whole((rows, wide))] * 2,
            [shaped((rows, wide), BF16)] * 2,
        )(meta, *received[c], c_input, bc_oth, inners[c], endb, end_oth)
        back.append(lax.ppermute(oth, "seq", swap))
        mixer_out = finish(mixer_out, side * count + c, own)
    for c in range(count):
        mixer_out = finish(mixer_out, (1 - side) * count + c, back[c])

    seg_len = rows * peers // segment_order.shape[0]

    def positions(block):
        at = block[:, None] * rows + jnp.arange(rows, dtype=jnp.int32)[None, :]
        at = at.reshape(-1)
        return segment_order[at // seg_len] * seg_len + at % seg_len

    every = jnp.arange(planes, dtype=jnp.int32) * 2
    key_pos = positions(jnp.concatenate([every + side, every + 1 - side]))[None, :]
    query_pos = positions(here[None])[:, None]
    kv_spec = lambda at, lead: pl.BlockSpec(
        (planes, rows, ATT_DIM), lambda g, m, at=at: (0, 0, at + g)
    )
    attn_out = call(
        functools.partial(attend_body, per_used),
        (used_heads,),
        [pl.BlockSpec((rows, per_used * ATT_DIM), lambda g, m: (0, g))]
        + [kv_spec(0, 0), kv_spec(0, 0), kv_spec(used_heads, 0), kv_spec(used_heads, 0)]
        + [whole(query_pos.shape), whole(key_pos.shape)],
        pl.BlockSpec((rows, per_used * ATT_DIM), lambda g, m: (0, g)),
        shaped(queries.shape, BF16),
        scratch=[pltpu.VMEM((rows, key_pos.shape[1]), F32)],
    )(
        jnp.zeros((1,), jnp.int32), queries, gathered, other_side, gathered, other_side,
        query_pos, key_pos,
    )
    return mixer_out, attn_out


def solution(mesh):
    tokens = ("groups", "seq")
    both = ("head", "sub")
    placed = (
        P(tokens, both), P(tokens, both), P(tokens, both), P(tokens, both),
        P(tokens, "head"), P(tokens, "head"), P(both), P(both),
        P(tokens, both), P(tokens, "head"), P(tokens, "head"), P("groups"),
    )
    return jax.shard_map(
        local,
        mesh=mesh,
        in_specs=placed,
        out_specs=(P(tokens, both), P(tokens, both)),
        check_vma=False,
    )
```

time: 1000 us -> 234 us (0.23)
  waiting for transfers between devices: 613 us -> 14.7 us
  Pallas kernels: 0 us -> 121 us
  other arithmetic: 147 us -> 32.1 us
  local copies, waits for them, and re-layouts: 131 us -> 17.3 us
  matrix products: 76.5 us -> 0 us
  starting transfers between devices: 0.12 us -> 45.8 us
  blocking collectives: 14.8 us -> 0 us
  between operations: 14 us -> 1.09 us
    all_gather x3 -> x0, waiting for transfers between devices: 612 us -> none  [the longest x1 608 us: entering_2(): lax.all_gather(part.astype(kind), axis)]
    pallas_call x0 -> x31, Pallas kernels: none -> 121 us  [the longest x8 25.6 us: finish(): call(gate_body, (1,), specs, columns, shaped((rows, heads * WIDTH), BF16)...]
    select_n x9 -> x1, other arithmetic: 110 us -> 0.6 us  [local(): group_of = lambda chunk: (base + chunk * per_chunk) // PER_GROUP]
    dynamic_slice x16 -> x3, local copies, waits for them, and re-layouts: 105 us -> 1.98 us  [the longest x1 0.99 us: local(): lax.dynamic_slice_in_dim(values, start, kv_wide, 1)]
    dot_general x9 -> x0, matrix products: 76.5 us -> none  [the longest x1 20.7 us: local(): jnp.einsum('cqhn,chnp->cqhp', c_heads, entering.astype(jnp.bfloat16), pre...]
    ppermute x0 -> x29, starting transfers between devices: none -> 45.8 us  [the longest x12 15.2 us: local(): lax.ppermute(sends[c], 'seq', [(2 * h + x, 2 * h + 2 + x) for x in range(...]
    add x2 -> x3, other arithmetic: 16.4 us -> 1.35 us  [the longest x2 1.27 us: positions(): return segment_order[at // seg_len] * seg_len + at % seg_len]
    all_gather x1 -> x0, blocking collectives: 14.8 us -> none  [entering_2(): lax.all_gather(part.astype(kind), axis)]
  transfers between devices with their start and end apart: 3 -> 29, of which waited for: 2 -> 3; matrix products, arithmetic and copies ran while one was open for 11% -> 17% of each run, Pallas kernels for 0% -> 51%
where the time goes in v1:
time: 234 us; the launch traced here: 232 us
  Pallas kernels  121 us (52%)
  starting transfers between devices  45.8 us (20%)
  other arithmetic  32.1 us (14%)
  local copies, waits for them, and re-layouts  17.3 us (7%)
  waiting for transfers between devices  14.7 us (6%)
    pallas_call x8, Pallas kernels, finish(): call(gate_body, (1,), specs, columns, shaped((rows, heads * WIDTH), BF16)...  25.6 us
    pallas_call x8, Pallas kernels, local(): call(hop_body, (1,), [whole((STATE, wide)), whole((STATE, wide)), narrow(...  25.1 us
    pallas_call x4, Pallas kernels, local(): call(plane_body, (1,), [columns, narrow(), narrow(), narrow(1), group_blo...  17.5 us
    ppermute x12, starting transfers between devices, local(): lax.ppermute(sends[c], 'seq', [(2 * h + x, 2 * h + 2 + x) for x in range(...  15.2 us
    ppermute x12, waiting for transfers between devices, local(): lax.ppermute(sends[c], 'seq', [(2 * h + x, 2 * h + 2 + x) for x in range(...  14.7 us
    pallas_call x1, Pallas kernels, local(): call(functools.partial(attend_body, per_used), (used_heads,), [pl.BlockSp...  14 us
    pallas_call x4, Pallas kernels, local(): call(functools.partial(carried_body, planes - 1), (1,), [whole((STATE, wi...  13.7 us
    pallas_call x4, Pallas kernels, local(): call(send_body, (1,), [columns, narrow(), narrow()], whole((rows, wide)),...  12.2 us
  transfers between devices with their start and end apart: 29, of which 3 were waited for; matrix products, arithmetic and copies ran while one was open for 17% of the time, Pallas kernels for 51%

profile of v1, /device:TPU:18, one launch (start us, length us, event | category | flops | bytes accessed | tf_op | source)
XLA Modules:
  0.0 232.3 jit_solution(7252914935500140143)
XLA Ops:
  2.4 3.5 %collective-permute-start.22 = (bf16[128,1024]{1,0:T(8,128)(2,1)}, bf16[128,1024]{1,0:T(8,128)(2,1)}, u32[]{:S(2)}, u32[]{:S(2)}) collective-permute-start(bf16[128,1024]{1,0:T(8,128)(2,1)} %pad_maximum_fusion.1), channel_id=1, source_target_pairs={{0,4},{2,6},{4,8},{6,10},{8,12},{10,14},{1,5},{3,7},{5,9},{7,11},{... | collective-permute-start | bytes 786440 | tf_op jit(solution)/shard_map/ppermute | solution.py:242
  23.6 4.6 %select_reduce_fusion = s32[128]{0:T(128)S(1)} fusion(s32[]{:T(128)} %bitcast.32, s32[]{:T(128)} %bitcast.33, s32[]{:T(128)} %bitcast.34, s32[]{:T(128)} %bitcast.35, s32[]{:T(128)} %bitcast.36, s32[]{:T(128)} %bitcast.38, s32[]{:T(128)} %bitcast.37, s32[]{:T(128)S(6)} %mul.112), kind=kLoop, calls=%fused_computation.16 | loop fusion | flops 3968 | bytes 544 | tf_op jit(solution)/shard_map/gather | solution.py:392
  28.3 4.5 %compare_select_fusion.4 = (s32[1024,1]{0,1:T(1,128)S(1)}, s32[1024,1]{0,1:T(1,128)S(1)}) fusion(s32[]{:T(128)} %bitcast.32, s32[]{:T(128)} %bitcast.33, s32[]{:T(128)} %bitcast.34, s32[]{:T(128)} %bitcast.35, s32[]{:T(128)} %bitcast.36, s32[]{:T(128)} %bitcast.38, s32[]{:T(128)} %bitcast.37, s32[1024,1]{0,1:T(1,128)S(1)} %bitcast.61), kind=kLoop, calls=%fused_computation.45 | loop fusion | flops 30720 | bytes 12316 | tf_op jit(solution)/shard_map/gather | solution.py:392
  32.8 5.8 %fusion.8 = s32[128,1]{0,1:T(1,128)S(1)} fusion(pred[128]{0:T(512)(128)(4,1)S(1)} %get-tuple-element.85, pred[128]{0:T(512)(128)(4,1)S(1)} %get-tuple-element.86, pred[128]{0:T(512)(128)(4,1)S(1)} %get-tuple-element.87, pred[128]{0:T(512)(128)(4,1)S(1)} %get-tuple-element.88, pred[128]{0:T(512)(128)(4,1)S(1)} %get-tuple-element.89, ...), kind=kLoop, calls=%fused_computation.83 | loop fusion | flops 1280 | bytes 2212 | tf_op jit(solution)/shard_map/mul | solution.py:392
  53.5 4.2 %collective-permute-start.24 = (bf16[128,1024]{1,0:T(8,128)(2,1)}, bf16[128,1024]{1,0:T(8,128)(2,1)}, u32[]{:S(2)}, u32[]{:S(2)}) collective-permute-start(bf16[128,1024]{1,0:T(8,128)(2,1)} %collective-permute-done.22), channel_id=1, source_target_pairs={{0,4},{2,6},{4,8},{6,10},{8,12},{10,14},{1,5},{3,7},{5,9},{7,11},{... | collective-permute-start | bytes 786440 | tf_op jit(solution)/shard_map/ppermute | solution.py:242
  58.4 4.4 %shard_map.134 = (f32[256,1024]{1,0:T(8,128)}, bf16[256,1024]{1,0:T(8,128)(2,1)}, f32[128,1024]{1,0:T(8,128)}) custom-call(s32[3]{0:T(128)} %pad_add_fusion.1.meta._, bf16[128,8192]{1,0:T(8,128)(2,1)} %x_ref.17, f32[8,128,16]{2,1,0:T(8,128)} %get-tuple-element.27.step_ref, f32[8,128,16]{2,1,0:T(8,128)} %get-tuple-element.30.w_ref, ...), custom_call_target="tpu_custom_call" | custom-call | tf_op jit(solution)/shard_map/pallas_call | solution.py:300
  66.7 4.4 %shard_map.139 = (f32[256,1024]{1,0:T(8,128)}, bf16[256,1024]{1,0:T(8,128)(2,1)}, f32[128,1024]{1,0:T(8,128)}) custom-call(s32[3]{0:T(128)} %pad_add_fusion.3.meta._, bf16[128,8192]{1,0:T(8,128)(2,1)} %x_ref.17, f32[8,128,16]{2,1,0:T(8,128)} %get-tuple-element.27.step_ref, f32[8,128,16]{2,1,0:T(8,128)} %get-tuple-element.30.w_ref, ...), custom_call_target="tpu_custom_call" | custom-call | tf_op jit(solution)/shard_map/pallas_call | solution.py:300
  72.6 4.4 %shard_map.144 = (f32[256,1024]{1,0:T(8,128)}, bf16[256,1024]{1,0:T(8,128)(2,1)}, f32[128,1024]{1,0:T(8,128)}) custom-call(s32[3]{0:T(128)} %pad_add_fusion.5.meta._, bf16[128,8192]{1,0:T(8,128)(2,1)} %x_ref.17, f32[8,128,16]{2,1,0:T(8,128)} %get-tuple-element.27.step_ref, f32[8,128,16]{2,1,0:T(8,128)} %get-tuple-element.30.w_ref, ...), custom_call_target="tpu_custom_call" | custom-call | tf_op jit(solution)/shard_map/pallas_call | solution.py:300
  77.7 4.4 %shard_map.149 = (f32[256,1024]{1,0:T(8,128)}, bf16[256,1024]{1,0:T(8,128)(2,1)}, f32[128,1024]{1,0:T(8,128)}) custom-call(s32[3]{0:T(128)} %pad_add_fusion.7.meta._, bf16[128,8192]{1,0:T(8,128)(2,1)} %x_ref.17, f32[8,128,16]{2,1,0:T(8,128)} %get-tuple-element.27.step_ref, f32[8,128,16]{2,1,0:T(8,128)} %get-tuple-element.30.w_ref, ...), custom_call_target="tpu_custom_call" | custom-call | tf_op jit(solution)/shard_map/pallas_call | solution.py:300
  83.8 4.3 %collective-permute-start.26 = (bf16[128,1024]{1,0:T(8,128)(2,1)}, bf16[128,1024]{1,0:T(8,128)(2,1)S(1)}, u32[]{:S(2)}, u32[]{:S(2)}) collective-permute-start(bf16[128,1024]{1,0:T(8,128)(2,1)} %collective-permute-done.24), channel_id=1, source_target_pairs={{0,4},{2,6},{4,8},{6,10},{8,12},{10,14},{1,5},{3,7},{5,9},{7,11},{... | collective-permute-start | bytes 786440 | tf_op jit(solution)/shard_map/ppermute | solution.py:242
  119.3 5.6 %collective-permute-done.9.recv_ref.refs_1_ = bf16[256,1024]{1,0:T(8,128)(2,1)} collective-permute-done((bf16[256,1024]{1,0:T(8,128)(2,1)}, bf16[256,1024]{1,0:T(8,128)(2,1)}, u32[]{:S(2)}, u32[]{:S(2)}) %collective-permute-start.9) | collective-permute-done | bytes 524320 | tf_op jit(solution)/shard_map/ppermute | solution.py:322
  129.4 6.8 %collective-permute-done.14.recv_ref.refs_1_ = bf16[256,1024]{1,0:T(8,128)(2,1)} collective-permute-done((bf16[256,1024]{1,0:T(8,128)(2,1)}, bf16[256,1024]{1,0:T(8,128)(2,1)}, u32[]{:S(2)}, u32[]{:S(2)}) %collective-permute-start.14) | collective-permute-done | bytes 524320 | tf_op jit(solution)/shard_map/ppermute | solution.py:322
  148.7 5.8 %select_multiply_fusion = s32[1024]{0:T(1024)S(1)} fusion(pred[1024]{0:T(1024)(128)(4,1)S(1)} %get-tuple-element.60, pred[1024]{0:T(1024)(128)(4,1)S(1)} %get-tuple-element.59, pred[1024]{0:T(1024)(128)(4,1)S(1)} %get-tuple-element.58, pred[1024]{0:T(1024)(128)(4,1)S(1)} %get-tuple-element.57, pred[1024]{0:T(1024)(128)(4,1)S(1)} %get-tuple-element.56, ...), kind=kLoop, calls=%fused_computation.58 | loop fusion | flops 10240 | bytes 17444 | tf_op jit(solution)/shard_map/mul | solution.py:392
  155.9 3.4 %shard_map.137 = (bf16[128,1024]{1,0:T(8,128)(2,1)}, bf16[128,1024]{1,0:T(8,128)(2,1)}) custom-call(s32[3]{0:T(128)} %pad_add_fusion.1.meta._, bf16[256,1024]{1,0:T(8,128)(2,1)} %copy-done.4, bf16[256,1024]{1,0:T(8,128)(2,1)} %collective-permute-done.4.recv_ref.refs_1_, bf16[256,1024]{1,0:T(8,128)(2,1)} %copy-done.11, bf16[128,2048]{1,0:T(8,128)(2,1)} %refs_3_.7, ...), custom_call_target="tpu_custom_call" | custom-call | tf_op jit(solution)/shard_map/pallas_call | solution.py:374
  160.6 3.4 %shard_map.142 = (bf16[128,1024]{1,0:T(8,128)(2,1)}, bf16[128,1024]{1,0:T(8,128)(2,1)}) custom-call(s32[3]{0:T(128)} %pad_add_fusion.3.meta._, bf16[256,1024]{1,0:T(8,128)(2,1)} %collective-permute-done.8.recv_ref.refs_0_, bf16[256,1024]{1,0:T(8,128)(2,1)} %collective-permute-done.9.recv_ref.refs_1_, bf16[256,1024]{1,0:T(8,128)(2,1)} %copy-done.10, ...), custom_call_target="tpu_custom_call" | custom-call | tf_op jit(solution)/shard_map/pallas_call | solution.py:374
  166.3 3.4 %shard_map.147 = (bf16[128,1024]{1,0:T(8,128)(2,1)}, bf16[128,1024]{1,0:T(8,128)(2,1)}) custom-call(s32[3]{0:T(128)} %pad_add_fusion.5.meta._, bf16[256,1024]{1,0:T(8,128)(2,1)} %copy-done.5, bf16[256,1024]{1,0:T(8,128)(2,1)} %collective-permute-done.14.recv_ref.refs_1_, bf16[256,1024]{1,0:T(8,128)(2,1)} %copy-done.9, bf16[128,2048]{1,0:T(8,128)(2,1)} %refs_3_.7, ...), custom_call_target="tpu_custom_call" | custom-call | tf_op jit(solution)/shard_map/pallas_call | solution.py:374
  171.1 3.5 %shard_map.152 = (bf16[128,1024]{1,0:T(8,128)(2,1)}, bf16[128,1024]{1,0:T(8,128)(2,1)}) custom-call(s32[3]{0:T(128)} %pad_add_fusion.7.meta._, bf16[256,1024]{1,0:T(8,128)(2,1)} %copy-done.3, bf16[256,1024]{1,0:T(8,128)(2,1)} %copy-done.6, bf16[256,1024]{1,0:T(8,128)(2,1)} %copy-done.8, bf16[128,2048]{1,0:T(8,128)(2,1)} %refs_3_.7, ...), custom_call_target="tpu_custom_call" | custom-call | tf_op jit(solution)/shard_map/pallas_call | solution.py:374
  177.5 10.7 %shard_map.132.mixed_ref = f32[128,8192]{1,0:T(8,128)} custom-call(s32[8]{0:T(128)} %and_select_fusion.2._, bf16[128,8192]{1,0:T(8,128)(2,1)} %x_ref.17, f32[8,128,16]{2,1,0:T(8,128)} %get-tuple-element.27.step_ref, f32[8,128,16]{2,1,0:T(8,128)} %get-tuple-element.28.cum_ref, f32[8,16,128]{2,1,0:T(8,128)} %bitcast.60, f32[8,1,16]{2,1,0:T(1,128)} %bitcast.63, ...), custom_call_target="tpu_custom_call" | custom-call | tf_op jit(solution)/shard_map/pallas_call | solution.py:334
  188.9 3.2 %shard_map.153.rest_0_ = bf16[128,8192]{1,0:T(8,128)(2,1)} custom-call(s32[2]{0:T(128)} %pad_add_fusion.11.meta, f32[128,8192]{1,0:T(8,128)} %shard_map.132.mixed_ref, bf16[128,1024]{1,0:T(8,128)(2,1)} %get-tuple-element.51.carried_ref, bf16[128,8192]{1,0:T(8,128)(2,1)} %gate_ref.15, f32[8,128,16]{2,1,0:T(8,128)} %get-tuple-element.28.cum_ref, ...), custom_call_target="tpu_custom_call" | custom-call | tf_op jit(solution)/shard_map/pallas_call | solution.py:367
  192.1 3.2 %shard_map.154.rest_0_ = bf16[128,8192]{1,0:T(8,128)(2,1)} custom-call(s32[2]{0:T(128)} %pad_add_fusion.10.meta, f32[128,8192]{1,0:T(8,128)} %shard_map.132.mixed_ref, bf16[128,1024]{1,0:T(8,128)(2,1)} %get-tuple-element.50.carried_ref, bf16[128,8192]{1,0:T(8,128)(2,1)} %gate_ref.15, ...), custom_call_target="tpu_custom_call", output_to_operand_aliasing={{}: (6, {})} | custom-call | tf_op jit(solution)/shard_map/pallas_call | solution.py:367
  195.3 3.2 %shard_map.155.rest_0_ = bf16[128,8192]{1,0:T(8,128)(2,1)} custom-call(s32[2]{0:T(128)} %pad_add_fusion.9.meta, f32[128,8192]{1,0:T(8,128)} %shard_map.132.mixed_ref, bf16[128,1024]{1,0:T(8,128)(2,1)} %get-tuple-element.49.carried_ref, bf16[128,8192]{1,0:T(8,128)(2,1)} %gate_ref.15, ...), custom_call_target="tpu_custom_call", output_to_operand_aliasing={{}: (6, {})} | custom-call | tf_op jit(solution)/shard_map/pallas_call | solution.py:367
  198.5 3.2 %shard_map.156.rest_0_ = bf16[128,8192]{1,0:T(8,128)(2,1)} custom-call(s32[2]{0:T(128)} %pad_add_fusion.8.meta, f32[128,8192]{1,0:T(8,128)} %shard_map.132.mixed_ref, bf16[128,1024]{1,0:T(8,128)(2,1)} %get-tuple-element.48.carried_ref, bf16[128,8192]{1,0:T(8,128)(2,1)} %gate_ref.15, ...), custom_call_target="tpu_custom_call", output_to_operand_aliasing={{}: (6, {})} | custom-call | tf_op jit(solution)/shard_map/pallas_call | solution.py:367
  202.7 14.0 %shard_map.161 = bf16[128,4096]{1,0:T(8,128)(2,1)} custom-call(s32[1]{0:T(128)} %constant.160.clone.1._, bf16[128,4096]{1,0:T(8,128)(2,1)} %q_ref.1, bf16[5,128,1024]{2,1,0:T(8,128)(2,1)} %copy-done.1, bf16[4,128,1024]{2,1,0:T(8,128)(2,1)} %copy-done.2, bf16[5,128,1024]{2,1,0:T(8,128)(2,1)} %copy-done.1, bf16[4,128,1024]{2,1,0:T(8,128)(2,1)} %copy-done.2, ...), custom_call_target="tpu_custom_call" | custom-call | tf_op jit(solution)/shard_map/pallas_call | solution.py:400
  229.1 3.2 %shard_map.160 = bf16[128,8192]{1,0:T(8,128)(2,1)} custom-call(s32[2]{0:T(128)} %pad_add_fusion._.meta, f32[128,8192]{1,0:T(8,128)} %shard_map.132.mixed_ref, bf16[128,1024]{1,0:T(8,128)(2,1)} %copy-done.19, bf16[128,8192]{1,0:T(8,128)(2,1)} %gate_ref.15, f32[8,128,16]{2,1,0:T(8,128)} %get-tuple-element.28.cum_ref, ...), custom_call_target="tpu_custom_call", output_to_operand_aliasing={{}: (6, {})} | custom-call | tf_op jit(solution)/shard_map/pallas_call | solution.py:367
  (160 shorter events, 114.1 us)
Async XLA Ops:
  2.4 51.2 %collective-permute-start.22 = (bf16[128,1024]{1,0:T(8,128)(2,1)}, bf16[128,1024]{1,0:T(8,128)(2,1)}, u32[]{:S(2)}, u32[]{:S(2)}) collective-permute-start(bf16[128,1024]{1,0:T(8,128)(2,1)} %pad_maximum_fusion.1), channel_id=1, source_target_pairs={{0,4},{2,6},{4,8},{6,10},{8,12},{10,14},{1,5},{3,7},{5,9},{7,11},{... | collective-permute-start | bytes 786440 | tf_op jit(solution)/shard_map/ppermute | solution.py:242
  5.9 57.6 %collective-permute-start.23 = (bf16[128,1024]{1,0:T(8,128)(2,1)}, bf16[128,1024]{1,0:T(8,128)(2,1)}, u32[]{:S(2)}, u32[]{:S(2)}) collective-permute-start(bf16[128,1024]{1,0:T(8,128)(2,1)} %pad_maximum_fusion.1), channel_id=1, source_target_pairs={{4,0},{6,2},{8,4},{10,6},{12,8},{14,10},{5,1},{7,3},{9,5},{11,7},{... | collective-permute-start | bytes 786440 | tf_op jit(solution)/shard_map/ppermute | solution.py:243
  14.6 36.0 %collective-permute-start = (bf16[128,1024]{1,0:T(8,128)(2,1)}, bf16[128,1024]{1,0:T(8,128)(2,1)S(1)}, u32[]{:S(2)}, u32[]{:S(2)}) collective-permute-start(bf16[128,1024]{1,0:T(8,128)(2,1)} %shard_map.133), channel_id=1, source_target_pairs={{0,2},{2,0},{4,6},{6,4},{8,10},{10,8},{12,14},{14,12},{1,3},{3,1},... | collective-permute-start | bytes 786440 | tf_op jit(solution)/shard_map/ppermute | solution.py:290
  16.2 35.8 %collective-permute-start.1 = (bf16[128,1024]{1,0:T(8,128)(2,1)S(1)}, bf16[128,1024]{1,0:T(8,128)(2,1)S(1)}, u32[]{:S(2)}, u32[]{:S(2)}) collective-permute-start(bf16[128,1024]{1,0:T(8,128)(2,1)S(1)} %pad_maximum_fusion), channel_id=1, source_target_pairs={{0,2},{2,0},{4,6},{6,4},{8,10},{10,8},{12,14},{14,12},{1,3},{3,1},... | collective-permute-start | bytes 786440 | tf_op jit(solution)/shard_map/ppermute | solution.py:266
  17.8 24.5 %collective-permute-start.2 = (f32[4,1,16]{2,1,0:T(1,128)S(1)}, f32[4,1,16]{2,1,0:T(1,128)S(1)}, u32[]{:S(2)}, u32[]{:S(2)}) collective-permute-start(f32[4,1,16]{2,1,0:T(1,128)S(1)} %constant_dynamic-slice_fusion.2), channel_id=1, source_target_pairs={{0,2},{2,0},{4,6},{6,4},{8,10},{10,8},{12,14},{14,12},{1,3},{3,1},... | collective-permute-start | bytes 776 | tf_op jit(solution)/shard_map/ppermute | solution.py:277
  52.0 25.0 %collective-permute-start.17 = (bf16[128,1024]{1,0:T(8,128)(2,1)S(1)}, bf16[128,1024]{1,0:T(8,128)(2,1)S(1)}, u32[]{:S(2)}, u32[]{:S(2)}) collective-permute-start(bf16[128,1024]{1,0:T(8,128)(2,1)S(1)} %copy-done.16), channel_id=1, source_target_pairs={{0,2},{2,0},{4,6},{6,4},{8,10},{10,8},{12,14},{14,12},{1,3},{3,1},... | collective-permute-start | bytes 786440 | tf_op jit(solution)/shard_map/ppermute | solution.py:290
  53.5 28.6 %collective-permute-start.24 = (bf16[128,1024]{1,0:T(8,128)(2,1)}, bf16[128,1024]{1,0:T(8,128)(2,1)}, u32[]{:S(2)}, u32[]{:S(2)}) collective-permute-start(bf16[128,1024]{1,0:T(8,128)(2,1)} %collective-permute-done.22), channel_id=1, source_target_pairs={{0,4},{2,6},{4,8},{6,10},{8,12},{10,14},{1,5},{3,7},{5,9},{7,11},{... | collective-permute-start | bytes 786440 | tf_op jit(solution)/shard_map/ppermute | solution.py:242
  62.8 26.3 %collective-permute-start.3 = (bf16[256,1024]{1,0:T(8,128)(2,1)}, bf16[256,1024]{1,0:T(8,128)(2,1)S(1)}, u32[]{:S(2)}, u32[]{:S(2)}) collective-permute-start(bf16[256,1024]{1,0:T(8,128)(2,1)} %get-tuple-element.32), channel_id=1, source_target_pairs={{0,4},{2,6},{1,5},{3,7},{16,20},{18,22},{17,21},{19,23}} | collective-permute-start | bytes 1572872 | tf_op jit(solution)/shard_map/ppermute | solution.py:322
  71.1 25.3 %collective-permute-start.8 = (bf16[256,1024]{1,0:T(8,128)(2,1)}, bf16[256,1024]{1,0:T(8,128)(2,1)}, u32[]{:S(2)}, u32[]{:S(2)}) collective-permute-start(bf16[256,1024]{1,0:T(8,128)(2,1)} %get-tuple-element.36), channel_id=1, source_target_pairs={{0,4},{2,6},{1,5},{3,7},{16,20},{18,22},{17,21},{19,23}} | collective-permute-start | bytes 1572872 | tf_op jit(solution)/shard_map/ppermute | solution.py:322
  77.0 23.9 %collective-permute-start.13 = (bf16[256,1024]{1,0:T(8,128)(2,1)}, bf16[256,1024]{1,0:T(8,128)(2,1)S(1)}, u32[]{:S(2)}, u32[]{:S(2)}) collective-permute-start(bf16[256,1024]{1,0:T(8,128)(2,1)} %get-tuple-element.40), channel_id=1, source_target_pairs={{0,4},{2,6},{1,5},{3,7},{16,20},{18,22},{17,21},{19,23}} | collective-permute-start | bytes 1572872 | tf_op jit(solution)/shard_map/ppermute | solution.py:322
  82.1 23.2 %collective-permute-start.18 = (bf16[256,1024]{1,0:T(8,128)(2,1)}, bf16[256,1024]{1,0:T(8,128)(2,1)S(1)}, u32[]{:S(2)}, u32[]{:S(2)}) collective-permute-start(bf16[256,1024]{1,0:T(8,128)(2,1)} %get-tuple-element.44), channel_id=1, source_target_pairs={{0,4},{2,6},{1,5},{3,7},{16,20},{18,22},{17,21},{19,23}} | collective-permute-start | bytes 1572872 | tf_op jit(solution)/shard_map/ppermute | solution.py:322
  83.8 26.1 %collective-permute-start.26 = (bf16[128,1024]{1,0:T(8,128)(2,1)}, bf16[128,1024]{1,0:T(8,128)(2,1)S(1)}, u32[]{:S(2)}, u32[]{:S(2)}) collective-permute-start(bf16[128,1024]{1,0:T(8,128)(2,1)} %collective-permute-done.24), channel_id=1, source_target_pairs={{0,4},{2,6},{4,8},{6,10},{8,12},{10,14},{1,5},{3,7},{5,9},{7,11},{... | collective-permute-start | bytes 786440 | tf_op jit(solution)/shard_map/ppermute | solution.py:242
  100.9 24.1 %collective-permute-start.9 = (bf16[256,1024]{1,0:T(8,128)(2,1)}, bf16[256,1024]{1,0:T(8,128)(2,1)}, u32[]{:S(2)}, u32[]{:S(2)}) collective-permute-start(bf16[256,1024]{1,0:T(8,128)(2,1)} %shard_map.140), channel_id=1, source_target_pairs={{4,8},{6,10},{5,9},{7,11},{20,24},{22,26},{21,25},{23,27}} | collective-permute-start | bytes 1572872 | tf_op jit(solution)/shard_map/ppermute | solution.py:322
  105.4 30.9 %collective-permute-start.14 = (bf16[256,1024]{1,0:T(8,128)(2,1)}, bf16[256,1024]{1,0:T(8,128)(2,1)}, u32[]{:S(2)}, u32[]{:S(2)}) collective-permute-start(bf16[256,1024]{1,0:T(8,128)(2,1)} %shard_map.145), channel_id=1, source_target_pairs={{4,8},{6,10},{5,9},{7,11},{20,24},{22,26},{21,25},{23,27}} | collective-permute-start | bytes 1572872 | tf_op jit(solution)/shard_map/ppermute | solution.py:322
  110.0 32.9 %collective-permute-start.19 = (bf16[256,1024]{1,0:T(8,128)(2,1)}, bf16[256,1024]{1,0:T(8,128)(2,1)S(1)}, u32[]{:S(2)}, u32[]{:S(2)}) collective-permute-start(bf16[256,1024]{1,0:T(8,128)(2,1)} %shard_map.150), channel_id=1, source_target_pairs={{4,8},{6,10},{5,9},{7,11},{20,24},{22,26},{21,25},{23,27}} | collective-permute-start | bytes 1572872 | tf_op jit(solution)/shard_map/ppermute | solution.py:322
  112.5 89.3 %collective-permute-start.28 = (bf16[4,128,1024]{2,1,0:T(8,128)(2,1)}, bf16[4,128,1024]{2,1,0:T(8,128)(2,1)S(1)}, u32[]{:S(2)}, u32[]{:S(2)}) collective-permute-start(bf16[4,128,1024]{2,1,0:T(8,128)(2,1)} %slice.38), channel_id=1, source_target_pairs={{0,2},{2,0},{4,6},{6,4},{8,10},{10,8},{12,14},{14,12},{1,3},{3,1},... | collective-permute-start | bytes 3145736 | tf_op jit(solution)/shard_map/ppermute | solution.py:250
  116.9 38.2 %collective-permute-start.5 = (bf16[256,1024]{1,0:T(8,128)(2,1)}, bf16[256,1024]{1,0:T(8,128)(2,1)S(1)}, u32[]{:S(2)}, u32[]{:S(2)}) collective-permute-start(bf16[256,1024]{1,0:T(8,128)(2,1)} %shard_map.136), channel_id=1, source_target_pairs={{8,12},{10,14},{9,13},{11,15},{24,28},{26,30},{25,29},{27,31}} | collective-permute-start | bytes 1572872 | tf_op jit(solution)/shard_map/ppermute | solution.py:322
  128.1 31.7 %collective-permute-start.10 = (bf16[256,1024]{1,0:T(8,128)(2,1)}, bf16[256,1024]{1,0:T(8,128)(2,1)S(1)}, u32[]{:S(2)}, u32[]{:S(2)}) collective-permute-start(bf16[256,1024]{1,0:T(8,128)(2,1)} %shard_map.141), channel_id=1, source_target_pairs={{8,12},{10,14},{9,13},{11,15},{24,28},{26,30},{25,29},{27,31}} | collective-permute-start | bytes 1572872 | tf_op jit(solution)/shard_map/ppermute | solution.py:322
  139.3 26.1 %collective-permute-start.15 = (bf16[256,1024]{1,0:T(8,128)(2,1)}, bf16[256,1024]{1,0:T(8,128)(2,1)S(1)}, u32[]{:S(2)}, u32[]{:S(2)}) collective-permute-start(bf16[256,1024]{1,0:T(8,128)(2,1)} %shard_map.146), channel_id=1, source_target_pairs={{8,12},{10,14},{9,13},{11,15},{24,28},{26,30},{25,29},{27,31}} | collective-permute-start | bytes 1572872 | tf_op jit(solution)/shard_map/ppermute | solution.py:322
  146.8 23.5 %collective-permute-start.20 = (bf16[256,1024]{1,0:T(8,128)(2,1)}, bf16[256,1024]{1,0:T(8,128)(2,1)S(1)}, u32[]{:S(2)}, u32[]{:S(2)}) collective-permute-start(bf16[256,1024]{1,0:T(8,128)(2,1)} %shard_map.151), channel_id=1, source_target_pairs={{8,12},{10,14},{9,13},{11,15},{24,28},{26,30},{25,29},{27,31}} | collective-permute-start | bytes 1572872 | tf_op jit(solution)/shard_map/ppermute | solution.py:322
  159.3 69.1 %collective-permute-start.6 = (bf16[128,1024]{1,0:T(8,128)(2,1)}, bf16[128,1024]{1,0:T(8,128)(2,1)S(1)}, u32[]{:S(2)}, u32[]{:S(2)}) collective-permute-start(bf16[128,1024]{1,0:T(8,128)(2,1)} %get-tuple-element.35), channel_id=1, source_target_pairs={{0,2},{2,0},{4,6},{6,4},{8,10},{10,8},{12,14},{14,12},{1,3},{3,1},... | collective-permute-start | bytes 786440 | tf_op jit(solution)/shard_map/ppermute | solution.py:382
  164.0 60.5 %collective-permute-start.11 = (bf16[128,1024]{1,0:T(8,128)(2,1)}, bf16[128,1024]{1,0:T(8,128)(2,1)S(1)}, u32[]{:S(2)}, u32[]{:S(2)}) collective-permute-start(bf16[128,1024]{1,0:T(8,128)(2,1)} %get-tuple-element.39), channel_id=1, source_target_pairs={{0,2},{2,0},{4,6},{6,4},{8,10},{10,8},{12,14},{14,12},{1,3},{3,1},... | collective-permute-start | bytes 786440 | tf_op jit(solution)/shard_map/ppermute | solution.py:382
  169.7 50.8 %collective-permute-start.16 = (bf16[128,1024]{1,0:T(8,128)(2,1)}, bf16[128,1024]{1,0:T(8,128)(2,1)S(1)}, u32[]{:S(2)}, u32[]{:S(2)}) collective-permute-start(bf16[128,1024]{1,0:T(8,128)(2,1)} %get-tuple-element.43), channel_id=1, source_target_pairs={{0,2},{2,0},{4,6},{6,4},{8,10},{10,8},{12,14},{14,12},{1,3},{3,1},... | collective-permute-start | bytes 786440 | tf_op jit(solution)/shard_map/ppermute | solution.py:382
  174.6 42.1 %collective-permute-start.21 = (bf16[128,1024]{1,0:T(8,128)(2,1)}, bf16[128,1024]{1,0:T(8,128)(2,1)S(1)}, u32[]{:S(2)}, u32[]{:S(2)}) collective-permute-start(bf16[128,1024]{1,0:T(8,128)(2,1)} %get-tuple-element.47), channel_id=1, source_target_pairs={{0,2},{2,0},{4,6},{6,4},{8,10},{10,8},{12,14},{14,12},{1,3},{3,1},... | collective-permute-start | bytes 786440 | tf_op jit(solution)/shard_map/ppermute | solution.py:382
  (30 other events, 170.6 us)

commit v2 on v1

v2 whole, which is shorter than its diff:
```python
import functools
import math
import jax
import jax.numpy as jnp
from jax import lax
from jax.experimental import pallas as pl
from jax.experimental.pallas import tpu as pltpu
from jax.sharding import PartitionSpec as P

SCAN_BLOCK = 128
MIXER_HEADS = 256
STATE = 256
GROUPS_BC = 8
ATT_HEADS = 64
KV_HEADS = 8
ATT_DIM = 128
WIDTH = 64
PER_GROUP = MIXER_HEADS // GROUPS_BC
CHUNKS = 4
SENDS = 2
SIDE, OWN, GIVEN, PLANE, GROUP = range(5)
F32 = jnp.float32
BF16 = jnp.bfloat16


def dot(a, b, dims=((1,), (0,))):
    return lax.dot_general(a, b, (dims, ((), ())), preferred_element_type=F32)


def pair_columns(cols, j):
    lane = lax.broadcasted_iota(jnp.int32, (cols.shape[0], 2 * WIDTH), 1)
    return jnp.where(lane < WIDTH, cols[:, 2 * j : 2 * j + 1], cols[:, 2 * j + 1 : 2 * j + 2])


def expand(cols):
    return jnp.concatenate([pair_columns(cols, j) for j in range(cols.shape[1] // 2)], axis=1)


def call(body, grid, in_specs, out_specs, out_shape, scratch=(), aliases={}):
    return pl.pallas_call(
        body,
        out_shape=out_shape,
        grid_spec=pltpu.PrefetchScalarGridSpec(
            num_scalar_prefetch=1,
            grid=grid,
            in_specs=in_specs,
            out_specs=out_specs,
            scratch_shapes=list(scratch),
        ),
        input_output_aliases=aliases,
    )


def shaped(shape, dtype):
    return jax.ShapeDtypeStruct(shape, dtype)


def whole(shape):
    zeros = (0,) * len(shape)
    return pl.BlockSpec(shape, lambda *_: zeros)


def scalars_body(_, step_ref, decay_ref, stepb, cumb, wb, endb, cumt):
    rows, heads = step_ref.shape
    chunks, width = stepb.shape[0], stepb.shape[2]
    decay = decay_ref[...]
    lower = (
        lax.broadcasted_iota(jnp.int32, (rows, rows), 0)
        >= lax.broadcasted_iota(jnp.int32, (rows, rows), 1)
    ).astype(F32)
    cum = lax.dot_general(
        lower, decay, (((1,), (0,)), ((), ())), precision=lax.Precision.HIGHEST,
        preferred_element_type=F32,
    )
    end = cum[rows - 1 : rows, :]
    w = jnp.exp(end - cum)
    factor = jnp.exp(end)
    cumt[...] = cum.T
    for j in range(chunks):
        cut = slice(j * width, (j + 1) * width)
        stepb[j] = step_ref[:, cut]
        cumb[j] = cum[:, cut]
        wb[j] = w[:, cut]
        endb[j] = factor[:, cut]


def weighted_inputs(x, step, w):
    parts = []
    for j in range(step.shape[1] // 2):
        cut = slice(j * 2 * WIDTH, (j + 1) * 2 * WIDTH)
        scaled = (x[:, cut].astype(F32) * pair_columns(step, j)).astype(BF16)
        parts.append((scaled.astype(F32) * pair_columns(w, j)).astype(BF16))
    return jnp.concatenate(parts, axis=1)


def send_body(_, x_ref, step_ref, w_ref, out_ref):
    out_ref[0] = weighted_inputs(x_ref[...], step_ref[0], w_ref[0])


def plane_body(
    meta, x_ref, step_ref, w_ref, end_ref, b_own, c_own, sd_oth, b_oth, c_oth, end_oth,
    total_ref, inner_ref, through_ref,
):
    first = meta[SIDE] == 0
    own = dot(b_own[...], weighted_inputs(x_ref[...], step_ref[0], w_ref[0]), ((0,), (0,)))
    oth = dot(b_oth[...], sd_oth[0], ((0,), (0,)))
    d_own, d_oth = expand(end_ref[0]), expand(end_oth[0])
    one = jnp.ones_like(d_own)
    total = own * jnp.where(first, d_oth, one) + oth * jnp.where(first, one, d_own)
    total_ref[...] = total.astype(BF16)
    through_ref[...] = d_own * d_oth
    earlier = jnp.where(first, own, oth).astype(BF16)
    c_later = jnp.where(first, c_oth[...].astype(F32), c_own[...].astype(F32)).astype(BF16)
    inner_ref[...] = dot(c_later, earlier).astype(BF16)


def carried_body(hops, meta, *refs):
    recvs = refs[:hops]
    c_own, c_oth, inner_ref, end_ref, end_oth, own_ref, oth_ref = refs[hops:]
    first = meta[SIDE] == 0
    state = recvs[0][...]
    for r in recvs[1:]:
        state = state + r[...]
    d_own, d_oth = expand(end_ref[0]), expand(end_oth[0])
    one = jnp.ones_like(d_own)
    inner = inner_ref[...].astype(F32)
    zero = jnp.zeros_like(inner)
    own = dot(c_own[...], state) * jnp.where(first, one, d_oth) + jnp.where(first, zero, inner)
    oth = dot(c_oth[...], state) * jnp.where(first, d_own, one) + jnp.where(first, inner, zero)
    own_ref[...] = own.astype(BF16)
    oth_ref[...] = oth.astype(BF16)


def within_body(_, x_ref, step_ref, cum_ref, cumt_ref, skip_ref, b_ref, c_ref, out_ref):
    rows = x_ref.shape[0]
    above = lax.broadcasted_iota(jnp.int32, (rows, rows), 0) < lax.broadcasted_iota(
        jnp.int32, (rows, rows), 1
    )
    inter = jnp.where(above, 0.0, dot(c_ref[...], b_ref[...], ((1,), (1,))))
    lane = lax.broadcasted_iota(jnp.int32, (rows, 2 * WIDTH), 1)
    step, cum, skip = step_ref[0], cum_ref[0], skip_ref[0]
    for j in range(step.shape[1] // 2):
        cut = slice(j * 2 * WIDTH, (j + 1) * 2 * WIDTH)
        x = x_ref[:, cut].astype(F32)
        scaled = x * pair_columns(step, j)
        weights = []
        for h in (2 * j, 2 * j + 1):
            gap = jnp.minimum(cum[:, h : h + 1] - cumt_ref[0, h : h + 1, :], 0.0)
            weights.append((jnp.exp(gap) * inter).astype(BF16))
        stacked = jnp.concatenate(
            [
                jnp.where(lane < WIDTH, scaled, 0.0).astype(BF16),
                jnp.where(lane < WIDTH, 0.0, scaled).astype(BF16),
            ],
            axis=0,
        )
        out_ref[:, cut] = dot(jnp.concatenate(weights, axis=1), stacked) + x * pair_columns(skip, j)


def gate_body(pieces, meta, mixed_ref, gate_ref, cum_ref, gain_ref, *rest):
    out_ref = rest[-1]
    size = 2 * WIDTH

    def run(carried_ref):
        cum = jnp.exp(cum_ref[0])
        same = (
            lax.broadcasted_iota(jnp.int32, (size, size), 0) // WIDTH
            == lax.broadcasted_iota(jnp.int32, (size, size), 1) // WIDTH
        )
        mean = jnp.where(same, 1.0 / WIDTH, 0.0).astype(BF16)
        for j in range(cum.shape[1] // 2):
            cut = slice(j * size, (j + 1) * size)
            mixed = mixed_ref[:, cut] + carried_ref[:, cut].astype(F32) * pair_columns(cum, j)
            gate = gate_ref[:, cut].astype(F32)
            gated = mixed * (gate / (1.0 + jnp.exp(-gate)))
            square = gated * gated
            high = square.astype(BF16)
            low = (square - high.astype(F32)).astype(BF16)
            mean_square = dot(high, mean) + dot(low, mean)
            normed = gated * lax.rsqrt(mean_square + 1e-05) * gain_ref[:, cut]
            out_ref[:, cut] = normed.astype(BF16)

    for k in range(pieces):
        pl.when(pl.program_id(0) == k)(functools.partial(run, rest[k]))


def attend_body(per_used, planes, seg_len, order_at, meta, q_ref, *refs):
    keys, values = refs[0:2], refs[2:4]
    out_ref, bias = refs[4:]
    rows, total_rows = bias.shape
    per_block = rows // seg_len

    @pl.when(pl.program_id(0) == 0)
    def _():
        lane = lax.broadcasted_iota(jnp.int32, (1, total_rows), 1)
        row = lax.broadcasted_iota(jnp.int32, (rows, 1), 0)
        key_pos, query_pos = lane, row
        side, plane = meta[SIDE], meta[PLANE]
        at = 0
        for turned in (0, 1):
            for i in range(planes):
                block = 2 * (plane ^ i) + (side ^ turned)
                for k in range(per_block):
                    origin = meta[order_at + block * per_block + k] * seg_len
                    key_pos = jnp.where(
                        lane // seg_len == at, origin + lane - at * seg_len, key_pos
                    )
                    if turned == 0 and i == 0:
                        query_pos = jnp.where(
                            row // seg_len == k, origin + row - k * seg_len, query_pos
                        )
                    at += 1
        bias[...] = jnp.where(key_pos <= query_pos, 0.0, -jnp.inf)

    shape = (-1, ATT_DIM)
    key = jnp.concatenate([k[...].reshape(shape) for k in keys], axis=0)
    value = jnp.concatenate([v[...].reshape(shape) for v in values], axis=0)
    factor = ATT_DIM ** (-0.5) * math.log2(math.e)
    for r in range(per_used):
        cut = slice(r * ATT_DIM, (r + 1) * ATT_DIM)
        scores = dot(q_ref[:, cut], key, ((1,), (1,))) + bias[...]
        peak = jnp.max(scores, axis=1, keepdims=True)
        expos = jnp.exp2((scores - peak) * factor)
        total = jnp.sum(expos, axis=1, keepdims=True)
        out_ref[:, cut] = (dot(expos.astype(BF16), value) / total).astype(BF16)


def local(
    ssm_input, gate_input, step, log_decay, b_input, c_input, d_skip, norm_gain,
    queries, keys, values, segment_order,
):
    rows, heads = step.shape
    peers, here = lax.axis_size("seq"), lax.axis_index("seq")
    sub_index = lax.axis_index("sub")
    planes = peers // 2
    side, plane = here % 2, here // 2
    half = heads // 2
    count = CHUNKS
    per_chunk = half // count
    wide = per_chunk * WIDTH
    chunks = 2 * count
    swap = [(i, i ^ 1) for i in range(peers)]

    base = sub_index * heads
    group_of = lambda chunk: (base + chunk * per_chunk) // PER_GROUP
    order_at = GROUP + chunks
    meta = jnp.concatenate(
        [
            jnp.stack([side, side * count, (1 - side) * count, plane]),
            group_of(jnp.arange(chunks, dtype=jnp.int32)),
            segment_order,
        ]
    )

    stepb, cumb, wb, endb, cumt = call(
        scalars_body,
        (1,),
        [whole((rows, heads))] * 2,
        [whole((chunks, rows, per_chunk))] * 3 + [whole((chunks, 1, per_chunk)), whole((heads, rows))],
        [shaped((chunks, rows, per_chunk), F32)] * 3
        + [shaped((chunks, 1, per_chunk), F32), shaped((heads, rows), F32)],
    )(meta, step, log_decay)

    def narrow(origin, c=0, size=rows):
        return pl.BlockSpec((1, size, per_chunk), lambda i, m: (m[origin] + c + i, 0, 0))

    def columns(origin, c=0, size=rows):
        return pl.BlockSpec((size, wide), lambda i, m: (0, m[origin] + c + i))

    per_send = count // SENDS
    sd_oth = []
    for k in range(SENDS):
        at = k * per_send
        sd = call(
            send_body, (per_send,),
            [columns(GIVEN, at), narrow(GIVEN, at), narrow(GIVEN, at)],
            pl.BlockSpec((1, rows, wide), lambda i, m: (i, 0, 0)),
            shaped((per_send, rows, wide), BF16),
        )(meta, ssm_input, stepb, wb)
        sd_oth.append(lax.ppermute(sd, "seq", swap))

    groups_half = max(1, half // PER_GROUP)
    bc_start = ((base + (1 - side) * half) // PER_GROUP) * STATE
    bc_oth = lax.ppermute(
        jnp.concatenate(
            [
                lax.dynamic_slice_in_dim(b_input, bc_start, groups_half * STATE, 1),
                lax.dynamic_slice_in_dim(c_input, bc_start, groups_half * STATE, 1),
            ],
            axis=1,
        ),
        "seq",
        swap,
    )
    end_oth = lax.ppermute(
        lax.dynamic_slice_in_dim(endb, (1 - side) * count, count, 0), "seq", swap
    )

    query_count = queries.shape[1] // ATT_DIM
    ratio = ATT_HEADS // KV_HEADS
    used_heads = max(1, query_count // ratio)
    per_used = query_count // used_heads
    kv_wide = used_heads * ATT_DIM
    start = (sub_index * query_count // ratio) * ATT_DIM
    pack = jnp.concatenate(
        [
            lax.dynamic_slice_in_dim(keys, start, kv_wide, 1),
            lax.dynamic_slice_in_dim(values, start, kv_wide, 1),
        ],
        axis=1,
    )
    this_side = jnp.stack(
        [pack]
        + [
            lax.ppermute(pack, "seq", [(s, 2 * ((s // 2) ^ i) + s % 2) for s in range(peers)])
            for i in range(1, planes)
        ]
    )
    other_side = lax.ppermute(this_side, "seq", swap)

    def own_group(c):
        return pl.BlockSpec((rows, STATE), lambda i, m: (0, m[GROUP + m[OWN] + c]))

    def oth_group(c, at=0):
        at = at + c * per_chunk // PER_GROUP
        return pl.BlockSpec((rows, STATE), lambda i, m: (0, at))

    def oth_end(c):
        return pl.BlockSpec((1, 1, per_chunk), lambda i, m: (c, 0, 0))

    totals, inners, throughs = [], [], []
    for c in range(count):
        at = c % per_send
        total, inner, through = call(
            plane_body,
            (1,),
            [
                columns(OWN, c), narrow(OWN, c), narrow(OWN, c), narrow(OWN, c, 1),
                own_group(c), own_group(c),
                pl.BlockSpec((1, rows, wide), lambda i, m, at=at: (at, 0, 0)),
                oth_group(c), oth_group(c, groups_half), oth_end(c),
            ],
            [whole((STATE, wide)), whole((rows, wide)), whole((1, wide))],
            [shaped((STATE, wide), BF16), shaped((rows, wide), BF16), shaped((1, wide), F32)],
        )(
            meta, ssm_input, stepb, wb, endb, b_input, c_input,
            sd_oth[c // per_send], bc_oth, bc_oth, end_oth,
        )
        totals.append(total)
        inners.append(inner)
        throughs.append(through)

    sends = list(totals)
    received = [[] for _ in range(count)]
    for wave in range(count + planes - 2):
        for h in range(planes - 1):
            c = wave - h
            if not 0 <= c < count:
                continue
            got = lax.ppermute(sends[c], "seq", [(2 * h + x, 2 * h + 2 + x) for x in range(2)])
            received[c].append(got)
            if h < planes - 2:
                sends[c] = (throughs[c] * got.astype(F32) + totals[c].astype(F32)).astype(BF16)

    mixed = call(
        within_body,
        (chunks,),
        [
            pl.BlockSpec((rows, wide), lambda i, m: (0, i)),
            pl.BlockSpec((1, rows, per_chunk), lambda i, m: (i, 0, 0)),
            pl.BlockSpec((1, rows, per_chunk), lambda i, m: (i, 0, 0)),
            pl.BlockSpec((1, per_chunk, rows), lambda i, m: (i, 0, 0)),
            pl.BlockSpec((1, 1, per_chunk), lambda i, m: (i, 0, 0)),
            pl.BlockSpec((rows, STATE), lambda i, m: (0, m[GROUP + i])),
            pl.BlockSpec((rows, STATE), lambda i, m: (0, m[GROUP + i])),
        ],
        pl.BlockSpec((rows, wide), lambda i, m: (0, i)),
        shaped((rows, heads * WIDTH), F32),
    )(
        meta, ssm_input, stepb, cumb, cumt.reshape(chunks, per_chunk, rows),
        d_skip.reshape(chunks, 1, per_chunk), b_input, c_input,
    )

    gains = norm_gain.reshape(1, heads * WIDTH)

    def finish(mixer_out, origin, first, pieces):
        at = functools.partial(columns, origin, first)
        specs = [at(), at(), narrow(origin, first), at(1)]
        specs += [whole((rows, wide))] * len(pieces)
        args = [mixed, gate_input, cumb, gains, *pieces]
        aliases = {}
        if mixer_out is not None:
            specs.append(pl.BlockSpec(memory_space=pl.ANY))
            args.append(mixer_out)
            aliases = {len(args): 0}
        return call(
            functools.partial(gate_body, len(pieces)), (len(pieces),), specs, at(),
            shaped((rows, heads * WIDTH), BF16), aliases=aliases,
        )(meta, *args)

    owns, back = [], []
    for c in range(count):
        own, oth = call(
            functools.partial(carried_body, planes - 1),
            (1,),
            [whole((STATE, wide))] * (planes - 1)
            + [
                own_group(c), oth_group(c, groups_half), whole((rows, wide)),
                narrow(OWN, c, 1), oth_end(c),
            ],
            [whole((rows, wide))] * 2,
            [shaped((rows, wide), BF16)] * 2,
        )(meta, *received[c], c_input, bc_oth, inners[c], endb, end_oth)
        owns.append(own)
        back.append(lax.ppermute(oth, "seq", swap))
    mixer_out = finish(None, OWN, 0, owns)
    mixer_out = finish(mixer_out, GIVEN, 0, back[: count // 2])
    mixer_out = finish(mixer_out, GIVEN, count // 2, back[count // 2 :])

    seg_len = rows * peers // segment_order.shape[0]

    def kv_spec(at):
        return pl.BlockSpec((planes, rows, ATT_DIM), lambda g, m: (0, 0, at + g))

    head_block = pl.BlockSpec((rows, per_used * ATT_DIM), lambda g, m: (0, g))
    attn_out = call(
        functools.partial(attend_body, per_used, planes, seg_len, order_at),
        (used_heads,),
        [head_block, kv_spec(0), kv_spec(0), kv_spec(used_heads), kv_spec(used_heads)],
        head_block,
        shaped(queries.shape, BF16),
        scratch=[pltpu.VMEM((rows, rows * peers), F32)],
    )(meta, queries, this_side, other_side, this_side, other_side)
    return mixer_out, attn_out


def solution(mesh):
    tokens = ("groups", "seq")
    both = ("head", "sub")
    placed = (
        P(tokens, both), P(tokens, both), P(tokens, both), P(tokens, both),
        P(tokens, "head"), P(tokens, "head"), P(both), P(both),
        P(tokens, both), P(tokens, "head"), P(tokens, "head"), P("groups"),
    )
    return jax.shard_map(
        local,
        mesh=mesh,
        in_specs=placed,
        out_specs=(P(tokens, both), P(tokens, both)),
        check_vma=False,
    )
```

time: 234 us -> 187 us (0.80)
  waiting for transfers between devices: 14.7 us -> 57.6 us
  Pallas kernels: 121 us -> 79.4 us
  other arithmetic: 32.1 us -> 7.86 us
  starting transfers between devices: 45.8 us -> 29.2 us
  local copies, waits for them, and re-layouts: 17.3 us -> 9.25 us
    pallas_call x25 -> x10, Pallas kernels: 94.4 us -> 52.3 us  [the longest x4 15.8 us: local(): call(plane_body, (1,), [columns(OWN, c), narrow(OWN, c), narrow(OWN, c),...]
    ppermute x7 -> x4, waiting for transfers between devices: 0.02 us -> 18.8 us  [the longest x3 18.8 us: local(): lax.ppermute(pack, 'seq', [(s, 2 * (s // 2 ^ i) + s % 2) for s in range(p...]
    ppermute x7 -> x4, starting transfers between devices: 20.3 us -> 4.38 us  [the longest x3 3.78 us: local(): lax.ppermute(pack, 'seq', [(s, 2 * (s // 2 ^ i) + s % 2) for s in range(p...]
    ppermute x12, waiting for transfers between devices: 14.7 us -> 27 us  [local(): lax.ppermute(sends[c], 'seq', [(2 * h + x, 2 * h + 2 + x) for x in range(...]
    ppermute x1, waiting for transfers between devices: 0.01 us -> 11.7 us  [local(): lax.ppermute(lax.dynamic_slice_in_dim(endb, (1 - side) * count, count, 0)...]
    mul x3 -> x0, other arithmetic: 11.7 us -> none  [the longest x2 11.6 us: positions(): return segment_order[at // seg_len] * seg_len + at % seg_len]
    gather x8 -> x0, other arithmetic: 9.99 us -> none  [positions(): return segment_order[at // seg_len] * seg_len + at % seg_len]
    convert_element_type x0 -> x8, other arithmetic: none -> 7.64 us  [local(): (throughs[c] * got.astype(F32) + totals[c].astype(F32)).astype(BF16)]
  transfers between devices with their start and end apart: 29 -> 24, of which waited for: 3 -> 7; matrix products, arithmetic and copies ran while one was open for 17% -> 5% of each run, Pallas kernels for 51% -> 37%
where the time goes in v2:
time: 187 us; the launch traced here: 184 us
  Pallas kernels  79.4 us (42%)
  waiting for transfers between devices  57.6 us (31%)
  starting transfers between devices  29.2 us (16%)
  local copies, waits for them, and re-layouts  9.25 us (5%)
  other arithmetic  7.86 us (4%)
    ppermute x12, waiting for transfers between devices, local(): lax.ppermute(sends[c], 'seq', [(2 * h + x, 2 * h + 2 + x) for x in range(...  27 us
    ppermute x3, waiting for transfers between devices, local(): lax.ppermute(pack, 'seq', [(s, 2 * (s // 2 ^ i) + s % 2) for s in range(p...  18.8 us
    ppermute x12, starting transfers between devices, local(): lax.ppermute(sends[c], 'seq', [(2 * h + x, 2 * h + 2 + x) for x in range(...  16.6 us
    pallas_call x4, Pallas kernels, local(): call(plane_body, (1,), [columns(OWN, c), narrow(OWN, c), narrow(OWN, c),...  15.8 us
    pallas_call x1, Pallas kernels, local(): call(functools.partial(attend_body, per_used, planes, seg_len, order_at),...  14.5 us
    pallas_call x3, Pallas kernels, finish(): call(functools.partial(gate_body, len(pieces)), (len(pieces),), specs, at...  14.4 us
    pallas_call x4, Pallas kernels, local(): call(functools.partial(carried_body, planes - 1), (1,), [whole((STATE, wi...  13.1 us
    ppermute x1, waiting for transfers between devices, local(): lax.ppermute(lax.dynamic_slice_in_dim(endb, (1 - side) * count, count, 0)...  11.7 us
  transfers between devices with their start and end apart: 24, of which 7 were waited for; matrix products, arithmetic and copies ran while one was open for 5% of the time, Pallas kernels for 37%

profile of v2, /device:TPU:18, one launch (start us, length us, event | category | flops | bytes accessed | tf_op | source)
XLA Modules:
  0.0 184.3 jit_solution(9524830295293013318)
XLA Ops:
  2.0 3.3 %shard_map.131 = (f32[8,128,16]{2,1,0:T(8,128)}, f32[8,128,16]{2,1,0:T(8,128)}, f32[8,128,16]{2,1,0:T(8,128)}, f32[8,1,16]{2,1,0:T(1,128)}, f32[128,128]{1,0:T(8,128)}) custom-call(s32[28]{0:T(128)} %concatenate.9._.meta, f32[128,128]{1,0:T(8,128)} %step_ref.1, f32[128,128]{1,0:T(8,128)} %decay_ref.1), custom_call_target="tpu_custom_call" | custom-call | tf_op jit(solution)/shard_map/pallas_call | solution.py:255
  5.3 3.9 %shard_map.138 = bf16[2,128,1024]{2,1,0:T(8,128)(2,1)} custom-call(s32[28]{0:T(128)} %concatenate.9._.meta, bf16[128,8192]{1,0:T(8,128)(2,1)} %x_ref.13, f32[8,128,16]{2,1,0:T(8,128)} %get-tuple-element.27.step_ref, f32[8,128,16]{2,1,0:T(8,128)} %get-tuple-element.30.w_ref), custom_call_target="tpu_custom_call" | custom-call | tf_op jit(solution)/shard_map/pallas_call | solution.py:274
  12.8 3.8 %shard_map.133 = bf16[2,128,1024]{2,1,0:T(8,128)(2,1)} custom-call(s32[28]{0:T(128)} %concatenate.9._.meta, bf16[128,8192]{1,0:T(8,128)(2,1)} %x_ref.13, f32[8,128,16]{2,1,0:T(8,128)} %get-tuple-element.27.step_ref, f32[8,128,16]{2,1,0:T(8,128)} %get-tuple-element.30.w_ref), custom_call_target="tpu_custom_call" | custom-call | tf_op jit(solution)/shard_map/pallas_call | solution.py:274
  18.1 11.7 %collective-permute-done.2.end_oth.refs_7_ = f32[4,1,16]{2,1,0:T(1,128)S(1)} collective-permute-done((f32[4,1,16]{2,1,0:T(1,128)S(1)}, f32[4,1,16]{2,1,0:T(1,128)S(1)}, u32[]{:S(2)}, u32[]{:S(2)}) %collective-permute-start.2) | collective-permute-done | bytes 288 | tf_op jit(solution)/shard_map/ppermute | solution.py:295
  31.3 4.0 %shard_map.141 = (bf16[256,1024]{1,0:T(8,128)(2,1)}, bf16[128,1024]{1,0:T(8,128)(2,1)}, f32[1,1024]{1,0:T(1,128)}) custom-call(s32[28]{0:T(128)} %concatenate.9._.meta, bf16[128,8192]{1,0:T(8,128)(2,1)} %x_ref.13, f32[8,128,16]{2,1,0:T(8,128)} %get-tuple-element.27.step_ref, f32[8,128,16]{2,1,0:T(8,128)} %get-tuple-element.30.w_ref, ...), custom_call_target="tpu_custom_call" | custom-call | tf_op jit(solution)/shard_map/pallas_call | solution.py:334
  39.8 3.9 %shard_map.139 = (bf16[256,1024]{1,0:T(8,128)(2,1)}, bf16[128,1024]{1,0:T(8,128)(2,1)}, f32[1,1024]{1,0:T(1,128)}) custom-call(s32[28]{0:T(128)} %concatenate.9._.meta, bf16[128,8192]{1,0:T(8,128)(2,1)} %x_ref.13, f32[8,128,16]{2,1,0:T(8,128)} %get-tuple-element.27.step_ref, f32[8,128,16]{2,1,0:T(8,128)} %get-tuple-element.30.w_ref, ...), custom_call_target="tpu_custom_call" | custom-call | tf_op jit(solution)/shard_map/pallas_call | solution.py:334
  43.8 3.1 %collective-permute-done.20 = bf16[128,1024]{1,0:T(8,128)(2,1)S(1)} collective-permute-done((bf16[128,1024]{1,0:T(8,128)(2,1)S(1)}, bf16[128,1024]{1,0:T(8,128)(2,1)S(1)}, u32[]{:S(2)}, u32[]{:S(2)}) %collective-permute-start.20) | collective-permute-done | bytes 262176 | tf_op jit(solution)/shard_map/ppermute | solution.py:315
  47.6 15.7 %collective-permute-done.21 = bf16[128,1024]{1,0:T(8,128)(2,1)S(1)} collective-permute-done((bf16[128,1024]{1,0:T(8,128)(2,1)S(1)}, bf16[128,1024]{1,0:T(8,128)(2,1)S(1)}, u32[]{:S(2)}, u32[]{:S(2)}) %collective-permute-start.21) | collective-permute-done | bytes 262176 | tf_op jit(solution)/shard_map/ppermute | solution.py:315
  64.0 4.0 %shard_map.136 = (bf16[256,1024]{1,0:T(8,128)(2,1)}, bf16[128,1024]{1,0:T(8,128)(2,1)}, f32[1,1024]{1,0:T(1,128)}) custom-call(s32[28]{0:T(128)} %concatenate.9._.meta, bf16[128,8192]{1,0:T(8,128)(2,1)} %x_ref.13, f32[8,128,16]{2,1,0:T(8,128)} %get-tuple-element.27.step_ref, f32[8,128,16]{2,1,0:T(8,128)} %get-tuple-element.30.w_ref, ...), custom_call_target="tpu_custom_call" | custom-call | tf_op jit(solution)/shard_map/pallas_call | solution.py:334
  69.5 4.0 %shard_map.134 = (bf16[256,1024]{1,0:T(8,128)(2,1)}, bf16[128,1024]{1,0:T(8,128)(2,1)}, f32[1,1024]{1,0:T(1,128)}) custom-call(s32[28]{0:T(128)} %concatenate.9._.meta, bf16[128,8192]{1,0:T(8,128)(2,1)} %x_ref.13, f32[8,128,16]{2,1,0:T(8,128)} %get-tuple-element.27.step_ref, f32[8,128,16]{2,1,0:T(8,128)} %get-tuple-element.30.w_ref, ...), custom_call_target="tpu_custom_call" | custom-call | tf_op jit(solution)/shard_map/pallas_call | solution.py:334
  84.1 8.4 %collective-permute-done.17.refs_1_ = bf16[256,1024]{1,0:T(8,128)(2,1)S(1)} collective-permute-done((bf16[256,1024]{1,0:T(8,128)(2,1)S(1)}, bf16[256,1024]{1,0:T(8,128)(2,1)S(1)}, u32[]{:S(2)}, u32[]{:S(2)}) %collective-permute-start.17) | collective-permute-done | bytes 524320 | tf_op jit(solution)/shard_map/ppermute | solution.py:360
  92.7 2.1 %collective-permute-start.18 = (bf16[256,1024]{1,0:T(8,128)(2,1)S(1)}, bf16[256,1024]{1,0:T(8,128)(2,1)}, u32[]{:S(2)}, u32[]{:S(2)}) collective-permute-start(bf16[256,1024]{1,0:T(8,128)(2,1)S(1)} %fusion.7), channel_id=1, source_target_pairs={{8,12},{10,14},{9,13},{11,15},{24,28},{26,30},{25,29},{27,31}} | collective-permute-start | bytes 1572872 | tf_op jit(solution)/shard_map/ppermute | solution.py:360
  94.8 8.9 %collective-permute-done.13.refs_1_ = bf16[256,1024]{1,0:T(8,128)(2,1)S(1)} collective-permute-done((bf16[256,1024]{1,0:T(8,128)(2,1)S(1)}, bf16[256,1024]{1,0:T(8,128)(2,1)S(1)}, u32[]{:S(2)}, u32[]{:S(2)}) %collective-permute-start.13) | collective-permute-done | bytes 524320 | tf_op jit(solution)/shard_map/ppermute | solution.py:360
  106.9 7.2 %collective-permute-done.8.refs_1_ = bf16[256,1024]{1,0:T(8,128)(2,1)S(1)} collective-permute-done((bf16[256,1024]{1,0:T(8,128)(2,1)S(1)}, bf16[256,1024]{1,0:T(8,128)(2,1)S(1)}, u32[]{:S(2)}, u32[]{:S(2)}) %collective-permute-start.8) | collective-permute-done | bytes 524320 | tf_op jit(solution)/shard_map/ppermute | solution.py:360
  117.2 2.5 %collective-permute-done.4.refs_1_ = bf16[256,1024]{1,0:T(8,128)(2,1)S(1)} collective-permute-done((bf16[256,1024]{1,0:T(8,128)(2,1)S(1)}, bf16[256,1024]{1,0:T(8,128)(2,1)S(1)}, u32[]{:S(2)}, u32[]{:S(2)}) %collective-permute-start.4) | collective-permute-done | bytes 524320 | tf_op jit(solution)/shard_map/ppermute | solution.py:360
  122.2 3.3 %shard_map.142 = (bf16[128,1024]{1,0:T(8,128)(2,1)}, bf16[128,1024]{1,0:T(8,128)(2,1)}) custom-call(s32[28]{0:T(128)} %concatenate.9._.meta, bf16[256,1024]{1,0:T(8,128)(2,1)} %copy-done.4, bf16[256,1024]{1,0:T(8,128)(2,1)} %copy-done.13, bf16[256,1024]{1,0:T(8,128)(2,1)} %collective-permute-done.18.refs_2_, bf16[128,2048]{1,0:T(8,128)(2,1)} %refs_3_.7, ...), custom_call_target="tpu_custom_call" | custom-call | tf_op jit(solution)/shard_map/pallas_call | solution.py:403
  127.0 3.2 %shard_map.140 = (bf16[128,1024]{1,0:T(8,128)(2,1)}, bf16[128,1024]{1,0:T(8,128)(2,1)}) custom-call(s32[28]{0:T(128)} %concatenate.9._.meta, bf16[256,1024]{1,0:T(8,128)(2,1)} %copy-done.5, bf16[256,1024]{1,0:T(8,128)(2,1)} %copy-done.11, bf16[256,1024]{1,0:T(8,128)(2,1)} %collective-permute-done.14.refs_2_, bf16[128,2048]{1,0:T(8,128)(2,1)} %refs_3_.7, ...), custom_call_target="tpu_custom_call" | custom-call | tf_op jit(solution)/shard_map/pallas_call | solution.py:403
  130.8 3.4 %shard_map.137 = (bf16[128,1024]{1,0:T(8,128)(2,1)}, bf16[128,1024]{1,0:T(8,128)(2,1)}) custom-call(s32[28]{0:T(128)} %concatenate.9._.meta, bf16[256,1024]{1,0:T(8,128)(2,1)} %collective-permute-done.7.refs_0_, bf16[256,1024]{1,0:T(8,128)(2,1)} %copy-done.10, bf16[256,1024]{1,0:T(8,128)(2,1)} %collective-permute-done.9.refs_2_, bf16[128,2048]{1,0:T(8,128)(2,1)} %refs_3_.7, ...), custom_call_target="tpu_custom_call" | custom-call | tf_op jit(solution)/shard_map/pallas_call | solution.py:403
  136.4 3.2 %shard_map.135 = (bf16[128,1024]{1,0:T(8,128)(2,1)}, bf16[128,1024]{1,0:T(8,128)(2,1)}) custom-call(s32[28]{0:T(128)} %concatenate.9._.meta, bf16[256,1024]{1,0:T(8,128)(2,1)} %copy-done.6, bf16[256,1024]{1,0:T(8,128)(2,1)} %copy-done.8, bf16[256,1024]{1,0:T(8,128)(2,1)} %copy-done.15, bf16[128,2048]{1,0:T(8,128)(2,1)} %refs_3_.7, ...), custom_call_target="tpu_custom_call" | custom-call | tf_op jit(solution)/shard_map/pallas_call | solution.py:403
  140.9 10.7 %shard_map.132.mixed_ref = f32[128,8192]{1,0:T(8,128)} custom-call(s32[28]{0:T(128)} %concatenate.9._.meta, bf16[128,8192]{1,0:T(8,128)(2,1)} %x_ref.13, f32[8,128,16]{2,1,0:T(8,128)} %get-tuple-element.27.step_ref, f32[8,128,16]{2,1,0:T(8,128)} %get-tuple-element.28.cum_ref, f32[8,16,128]{2,1,0:T(8,128)} %bitcast.22, f32[8,1,16]{2,1,0:T(1,128)} %bitcast.31, ...), custom_call_target="tpu_custom_call" | custom-call | tf_op jit(solution)/shard_map/pallas_call | solution.py:365
  152.6 14.5 %shard_map.146 = bf16[128,4096]{1,0:T(8,128)(2,1)} custom-call(s32[28]{0:T(128)} %concatenate.9._.meta, bf16[128,4096]{1,0:T(8,128)(2,1)} %q_ref.1, bf16[4,128,1024]{2,1,0:T(8,128)(2,1)} %copy-done.1, bf16[4,128,1024]{2,1,0:T(8,128)(2,1)} %copy-done.2, bf16[4,128,1024]{2,1,0:T(8,128)(2,1)} %copy-done.1, bf16[4,128,1024]{2,1,0:T(8,128)(2,1)} %copy-done.2), custom_call_target="tpu_custom_call" | custom-call | tf_op jit(solution)/shard_map/pallas_call | solution.py:426
  167.0 6.2 %shard_map.143.rest_2_ = bf16[128,8192]{1,0:T(8,128)(2,1)} custom-call(s32[28]{0:T(128)} %concatenate.9._.meta, f32[128,8192]{1,0:T(8,128)} %shard_map.132.mixed_ref, bf16[128,8192]{1,0:T(8,128)(2,1)} %gate_ref.5, f32[8,128,16]{2,1,0:T(8,128)} %get-tuple-element.28.cum_ref, f32[1,8192]{1,0:T(1,128)} %bitcast.16, ...), custom_call_target="tpu_custom_call" | custom-call | tf_op jit(solution)/shard_map/pallas_call | solution.py:396
  174.7 4.1 %shard_map.144.rest_2_ = bf16[128,8192]{1,0:T(8,128)(2,1)} custom-call(s32[28]{0:T(128)} %concatenate.9._.meta, f32[128,8192]{1,0:T(8,128)} %shard_map.132.mixed_ref, bf16[128,8192]{1,0:T(8,128)(2,1)} %gate_ref.5, f32[8,128,16]{2,1,0:T(8,128)} %get-tuple-element.28.cum_ref, f32[1,8192]{1,0:T(1,128)} %bitcast.17, ...), custom_call_target="tpu_custom_call", output_to_operand_aliasing={{}: (7, {})} | custom-call | tf_op jit(solution)/shard_map/pallas_call | solution.py:396
  180.2 4.1 %shard_map.145 = bf16[128,8192]{1,0:T(8,128)(2,1)} custom-call(s32[28]{0:T(128)} %concatenate.9._.meta, f32[128,8192]{1,0:T(8,128)} %shard_map.132.mixed_ref, bf16[128,8192]{1,0:T(8,128)(2,1)} %gate_ref.5, f32[8,128,16]{2,1,0:T(8,128)} %get-tuple-element.28.cum_ref, f32[1,8192]{1,0:T(1,128)} %bitcast.18, ...), custom_call_target="tpu_custom_call", output_to_operand_aliasing={{}: (7, {})} | custom-call | tf_op jit(solution)/shard_map/pallas_call | solution.py:396
  (115 shorter events, 44.2 us)
Async XLA Ops:
  9.1 20.7 %collective-permute-start.11 = (bf16[2,128,1024]{2,1,0:T(8,128)(2,1)}, bf16[2,128,1024]{2,1,0:T(8,128)(2,1)S(1)}, u32[]{:S(2)}, u32[]{:S(2)}) collective-permute-start(bf16[2,128,1024]{2,1,0:T(8,128)(2,1)} %shard_map.138), channel_id=1, source_target_pairs={{0,2},{2,0},{4,6},{6,4},{8,10},{10,8},{12,14},{14,12},{1,3},{3,1},... | collective-permute-start | bytes 1572872 | tf_op jit(solution)/shard_map/ppermute | solution.py:280
  10.7 19.1 %collective-permute-start.1 = (bf16[128,1024]{1,0:T(8,128)(2,1)S(1)}, bf16[128,1024]{1,0:T(8,128)(2,1)S(1)}, u32[]{:S(2)}, u32[]{:S(2)}) collective-permute-start(bf16[128,1024]{1,0:T(8,128)(2,1)S(1)} %pad_maximum_fusion.1), channel_id=1, source_target_pairs={{0,2},{2,0},{4,6},{6,4},{8,10},{10,8},{12,14},{14,12},{1,3},{3,1},... | collective-permute-start | bytes 786440 | tf_op jit(solution)/shard_map/ppermute | solution.py:284
  12.3 17.5 %collective-permute-start.2 = (f32[4,1,16]{2,1,0:T(1,128)S(1)}, f32[4,1,16]{2,1,0:T(1,128)S(1)}, u32[]{:S(2)}, u32[]{:S(2)}) collective-permute-start(f32[4,1,16]{2,1,0:T(1,128)S(1)} %constant_dynamic-slice_fusion.2), channel_id=1, source_target_pairs={{0,2},{2,0},{4,6},{6,4},{8,10},{10,8},{12,14},{14,12},{1,3},{3,1},... | collective-permute-start | bytes 776 | tf_op jit(solution)/shard_map/ppermute | solution.py:295
  16.6 47.5 %collective-permute-start = (bf16[2,128,1024]{2,1,0:T(8,128)(2,1)}, bf16[2,128,1024]{2,1,0:T(8,128)(2,1)}, u32[]{:S(2)}, u32[]{:S(2)}) collective-permute-start(bf16[2,128,1024]{2,1,0:T(8,128)(2,1)} %shard_map.133), channel_id=1, source_target_pairs={{0,2},{2,0},{4,6},{6,4},{8,10},{10,8},{12,14},{14,12},{1,3},{3,1},... | collective-permute-start | bytes 1572872 | tf_op jit(solution)/shard_map/ppermute | solution.py:280
  35.3 39.0 %collective-permute-start.16 = (bf16[256,1024]{1,0:T(8,128)(2,1)}, bf16[256,1024]{1,0:T(8,128)(2,1)S(1)}, u32[]{:S(2)}, u32[]{:S(2)}) collective-permute-start(bf16[256,1024]{1,0:T(8,128)(2,1)} %get-tuple-element.44), channel_id=1, source_target_pairs={{0,4},{2,6},{1,5},{3,7},{16,20},{18,22},{17,21},{19,23}} | collective-permute-start | bytes 1572872 | tf_op jit(solution)/shard_map/ppermute | solution.py:360
  36.0 10.8 %collective-permute-start.20 = (bf16[128,1024]{1,0:T(8,128)(2,1)S(1)}, bf16[128,1024]{1,0:T(8,128)(2,1)S(1)}, u32[]{:S(2)}, u32[]{:S(2)}) collective-permute-start(bf16[128,1024]{1,0:T(8,128)(2,1)S(1)} %get-tuple-element.53), channel_id=1, source_target_pairs={{0,4},{2,6},{4,0},{6,2},{8,12},{10,14},{12,8},{14,10},{1,5},{3,7},... | collective-permute-start | bytes 786440 | tf_op jit(solution)/shard_map/ppermute | solution.py:315
  37.7 25.6 %collective-permute-start.21 = (bf16[128,1024]{1,0:T(8,128)(2,1)S(1)}, bf16[128,1024]{1,0:T(8,128)(2,1)S(1)}, u32[]{:S(2)}, u32[]{:S(2)}) collective-permute-start(bf16[128,1024]{1,0:T(8,128)(2,1)S(1)} %get-tuple-element.53), channel_id=1, source_target_pairs={{0,8},{2,10},{4,12},{6,14},{8,0},{10,2},{12,4},{14,6},{1,9},{3,11}... | collective-permute-start | bytes 786440 | tf_op jit(solution)/shard_map/ppermute | solution.py:315
  39.3 24.0 %collective-permute-start.22 = (bf16[128,1024]{1,0:T(8,128)(2,1)S(1)}, bf16[128,1024]{1,0:T(8,128)(2,1)S(1)}, u32[]{:S(2)}, u32[]{:S(2)}) collective-permute-start(bf16[128,1024]{1,0:T(8,128)(2,1)S(1)} %get-tuple-element.53), channel_id=1, source_target_pairs={{0,12},{2,14},{4,8},{6,10},{8,4},{10,6},{12,0},{14,2},{1,13},{3,15... | collective-permute-start | bytes 786440 | tf_op jit(solution)/shard_map/ppermute | solution.py:315
  46.9 30.3 %collective-permute-start.12 = (bf16[256,1024]{1,0:T(8,128)(2,1)}, bf16[256,1024]{1,0:T(8,128)(2,1)S(1)}, u32[]{:S(2)}, u32[]{:S(2)}) collective-permute-start(bf16[256,1024]{1,0:T(8,128)(2,1)} %get-tuple-element.40), channel_id=1, source_target_pairs={{0,4},{2,6},{1,5},{3,7},{16,20},{18,22},{17,21},{19,23}} | collective-permute-start | bytes 1572872 | tf_op jit(solution)/shard_map/ppermute | solution.py:360
  63.4 88.1 %collective-permute-start.23 = (bf16[4,128,1024]{2,1,0:T(8,128)(2,1)S(1)}, bf16[4,128,1024]{2,1,0:T(8,128)(2,1)S(1)}, u32[]{:S(2)}, u32[]{:S(2)}) collective-permute-start(bf16[4,128,1024]{2,1,0:T(8,128)(2,1)S(1)} %pad_maximum_fusion.refs_0_.refs_2_), channel_id=1, source_target_pairs={{0,2},{2,0},{4,6},{6,4},{8,10},{10,8},{12,14},{14,12},{1,3},{3,1},... | collective-permute-start | bytes 3145736 | tf_op jit(solution)/shard_map/ppermute | solution.py:319
  68.0 11.9 %collective-permute-start.7 = (bf16[256,1024]{1,0:T(8,128)(2,1)}, bf16[256,1024]{1,0:T(8,128)(2,1)}, u32[]{:S(2)}, u32[]{:S(2)}) collective-permute-start(bf16[256,1024]{1,0:T(8,128)(2,1)} %get-tuple-element.36), channel_id=1, source_target_pairs={{0,4},{2,6},{1,5},{3,7},{16,20},{18,22},{17,21},{19,23}} | collective-permute-start | bytes 1572872 | tf_op jit(solution)/shard_map/ppermute | solution.py:360
  73.5 9.1 %collective-permute-start.3 = (bf16[256,1024]{1,0:T(8,128)(2,1)}, bf16[256,1024]{1,0:T(8,128)(2,1)S(1)}, u32[]{:S(2)}, u32[]{:S(2)}) collective-permute-start(bf16[256,1024]{1,0:T(8,128)(2,1)} %get-tuple-element.32), channel_id=1, source_target_pairs={{0,4},{2,6},{1,5},{3,7},{16,20},{18,22},{17,21},{19,23}} | collective-permute-start | bytes 1572872 | tf_op jit(solution)/shard_map/ppermute | solution.py:360
  75.8 16.7 %collective-permute-start.17 = (bf16[256,1024]{1,0:T(8,128)(2,1)S(1)}, bf16[256,1024]{1,0:T(8,128)(2,1)S(1)}, u32[]{:S(2)}, u32[]{:S(2)}) collective-permute-start(bf16[256,1024]{1,0:T(8,128)(2,1)S(1)} %fusion.6), channel_id=1, source_target_pairs={{4,8},{6,10},{5,9},{7,11},{20,24},{22,26},{21,25},{23,27}} | collective-permute-start | bytes 1572872 | tf_op jit(solution)/shard_map/ppermute | solution.py:360
  78.6 25.1 %collective-permute-start.13 = (bf16[256,1024]{1,0:T(8,128)(2,1)S(1)}, bf16[256,1024]{1,0:T(8,128)(2,1)S(1)}, u32[]{:S(2)}, u32[]{:S(2)}) collective-permute-start(bf16[256,1024]{1,0:T(8,128)(2,1)S(1)} %fusion.4), channel_id=1, source_target_pairs={{4,8},{6,10},{5,9},{7,11},{20,24},{22,26},{21,25},{23,27}} | collective-permute-start | bytes 1572872 | tf_op jit(solution)/shard_map/ppermute | solution.py:360
  81.3 32.8 %collective-permute-start.8 = (bf16[256,1024]{1,0:T(8,128)(2,1)S(1)}, bf16[256,1024]{1,0:T(8,128)(2,1)S(1)}, u32[]{:S(2)}, u32[]{:S(2)}) collective-permute-start(bf16[256,1024]{1,0:T(8,128)(2,1)S(1)} %fusion.2), channel_id=1, source_target_pairs={{4,8},{6,10},{5,9},{7,11},{20,24},{22,26},{21,25},{23,27}} | collective-permute-start | bytes 1572872 | tf_op jit(solution)/shard_map/ppermute | solution.py:360
  82.8 36.9 %collective-permute-start.4 = (bf16[256,1024]{1,0:T(8,128)(2,1)S(1)}, bf16[256,1024]{1,0:T(8,128)(2,1)S(1)}, u32[]{:S(2)}, u32[]{:S(2)}) collective-permute-start(bf16[256,1024]{1,0:T(8,128)(2,1)S(1)} %fusion), channel_id=1, source_target_pairs={{4,8},{6,10},{5,9},{7,11},{20,24},{22,26},{21,25},{23,27}} | collective-permute-start | bytes 1572872 | tf_op jit(solution)/shard_map/ppermute | solution.py:360
  92.7 29.5 %collective-permute-start.18 = (bf16[256,1024]{1,0:T(8,128)(2,1)S(1)}, bf16[256,1024]{1,0:T(8,128)(2,1)}, u32[]{:S(2)}, u32[]{:S(2)}) collective-permute-start(bf16[256,1024]{1,0:T(8,128)(2,1)S(1)} %fusion.7), channel_id=1, source_target_pairs={{8,12},{10,14},{9,13},{11,15},{24,28},{26,30},{25,29},{27,31}} | collective-permute-start | bytes 1572872 | tf_op jit(solution)/shard_map/ppermute | solution.py:360
  104.8 22.2 %collective-permute-start.14 = (bf16[256,1024]{1,0:T(8,128)(2,1)}, bf16[256,1024]{1,0:T(8,128)(2,1)}, u32[]{:S(2)}, u32[]{:S(2)}) collective-permute-start(bf16[256,1024]{1,0:T(8,128)(2,1)} %fusion.5), channel_id=1, source_target_pairs={{8,12},{10,14},{9,13},{11,15},{24,28},{26,30},{25,29},{27,31}} | collective-permute-start | bytes 1572872 | tf_op jit(solution)/shard_map/ppermute | solution.py:360
  115.1 15.6 %collective-permute-start.9 = (bf16[256,1024]{1,0:T(8,128)(2,1)}, bf16[256,1024]{1,0:T(8,128)(2,1)}, u32[]{:S(2)}, u32[]{:S(2)}) collective-permute-start(bf16[256,1024]{1,0:T(8,128)(2,1)} %fusion.3), channel_id=1, source_target_pairs={{8,12},{10,14},{9,13},{11,15},{24,28},{26,30},{25,29},{27,31}} | collective-permute-start | bytes 1572872 | tf_op jit(solution)/shard_map/ppermute | solution.py:360
  120.7 14.9 %collective-permute-start.5 = (bf16[256,1024]{1,0:T(8,128)(2,1)}, bf16[256,1024]{1,0:T(8,128)(2,1)S(1)}, u32[]{:S(2)}, u32[]{:S(2)}) collective-permute-start(bf16[256,1024]{1,0:T(8,128)(2,1)} %fusion.1), channel_id=1, source_target_pairs={{8,12},{10,14},{9,13},{11,15},{24,28},{26,30},{25,29},{27,31}} | collective-permute-start | bytes 1572872 | tf_op jit(solution)/shard_map/ppermute | solution.py:360
  125.5 47.8 %collective-permute-start.19 = (bf16[128,1024]{1,0:T(8,128)(2,1)}, bf16[128,1024]{1,0:T(8,128)(2,1)S(1)}, u32[]{:S(2)}, u32[]{:S(2)}) collective-permute-start(bf16[128,1024]{1,0:T(8,128)(2,1)} %get-tuple-element.47), channel_id=1, source_target_pairs={{0,2},{2,0},{4,6},{6,4},{8,10},{10,8},{12,14},{14,12},{1,3},{3,1},... | collective-permute-start | bytes 786440 | tf_op jit(solution)/shard_map/ppermute | solution.py:415
  130.2 43.1 %collective-permute-start.15 = (bf16[128,1024]{1,0:T(8,128)(2,1)}, bf16[128,1024]{1,0:T(8,128)(2,1)S(1)}, u32[]{:S(2)}, u32[]{:S(2)}) collective-permute-start(bf16[128,1024]{1,0:T(8,128)(2,1)} %get-tuple-element.43), channel_id=1, source_target_pairs={{0,2},{2,0},{4,6},{6,4},{8,10},{10,8},{12,14},{14,12},{1,3},{3,1},... | collective-permute-start | bytes 786440 | tf_op jit(solution)/shard_map/ppermute | solution.py:415
  134.1 44.7 %collective-permute-start.10 = (bf16[128,1024]{1,0:T(8,128)(2,1)}, bf16[128,1024]{1,0:T(8,128)(2,1)S(1)}, u32[]{:S(2)}, u32[]{:S(2)}) collective-permute-start(bf16[128,1024]{1,0:T(8,128)(2,1)} %get-tuple-element.39), channel_id=1, source_target_pairs={{0,2},{2,0},{4,6},{6,4},{8,10},{10,8},{12,14},{14,12},{1,3},{3,1},... | collective-permute-start | bytes 786440 | tf_op jit(solution)/shard_map/ppermute | solution.py:415
  139.7 39.1 %collective-permute-start.6 = (bf16[128,1024]{1,0:T(8,128)(2,1)}, bf16[128,1024]{1,0:T(8,128)(2,1)S(1)}, u32[]{:S(2)}, u32[]{:S(2)}) collective-permute-start(bf16[128,1024]{1,0:T(8,128)(2,1)} %get-tuple-element.35), channel_id=1, source_target_pairs={{0,2},{2,0},{4,6},{6,4},{8,10},{10,8},{12,14},{14,12},{1,3},{3,1},... | collective-permute-start | bytes 786440 | tf_op jit(solution)/shard_map/ppermute | solution.py:415
  (29 other events, 212.4 us)
